TPU v7x, 32 devices: a whole 2x2x4 slice. The times are simulated.
32 devices in a mesh: sec: 8 (over y, x, core), ch: 4 (over z).
Axes of the slice: x: 2, y: 2, z: 4, core: 2. Of those that a mesh axis runs over, the one named last changes fastest.
Arguments:
- start_amps: bfloat16 [6, 1024, 2048], P(None, 'ch'), may hold values from -6 to 6
- energies: float32 [6], replicated, may hold values from 0.5 to 2
- thresholds: bfloat16 [8, 1024], P('sec', 'ch'), may hold values from -3 to -1
- intersection: bfloat16 [8, 1024, 1024], P('sec', 'ch'), may hold values from -0.2 to 1
Outputs:
- boundary_amps: bfloat16 [8, 6, 1024, 2048], P('sec', None, 'ch')
All inputs are finite; a program needn't handle non-finite values.
Results may differ from a plain program's by a relative error of at most 0.04.
Values may be sent and summed in bfloat16 or wider, within the bound.
A program may use at most 64 MiB of HBM per device.

v0:
```python
import functools
import jax
import jax.numpy as jnp
from jax import lax
from jax.experimental import pallas as pl
from jax.experimental.pallas import tpu as pltpu
from jax.sharding import PartitionSpec as P


def passed_along(value, axis, steps):
    count = lax.axis_size(axis)
    leading, last = (max(0, -steps), min(count, count - steps))
    return lax.ppermute(value, axis, [(source, source + steps) for source in range(leading, last)])


def per_device_pipelined(start_amps, energies, thresholds, intersection):
    sectors = lax.axis_size("sec")
    sector_index = lax.axis_index("sec")
    groups = lax.axis_size("ch")
    energy_count = energies.shape[0]
    step_count = sectors + energy_count - 1
    row_count = intersection.shape[1]
    width_cols = start_amps.shape[2]
    half_cols = width_cols // 2
    col_width = half_cols // groups
    intersection_whole, thresholds_whole = (
        lax.all_gather(intersection, "ch", axis=1, tiled=True),
        lax.all_gather(thresholds, "ch", axis=1, tiled=True),
    )
    basis_change = intersection_whole[0]
    channel_thresholds = thresholds_whole[0].astype(jnp.float32)
    channel_count = basis_change.shape[0]
    paired = start_amps.reshape(energy_count, row_count, 2, half_cols)
    start_cols = lax.all_to_all(paired, "ch", split_axis=3, concat_axis=1, tiled=True)
    stored_init = jnp.zeros((energy_count, channel_count, 2, col_width), jnp.bfloat16)

    def multiply(flat):
        return jnp.dot(basis_change, flat, preferred_element_type=jnp.float32).astype(jnp.bfloat16)

    def skipped(flat):
        return jnp.zeros((channel_count, 2 * col_width), jnp.bfloat16)

    def step(step_index, state_pair):
        outgoing, stored = state_pair
        incoming = passed_along(outgoing, "sec", 1)
        energy_raw = step_index - sector_index
        active = (energy_raw >= 0) & (energy_raw < energy_count)
        energy_slot = jnp.clip(energy_raw, 0, energy_count - 1)
        initial = lax.dynamic_index_in_dim(start_cols, energy_slot, 0, keepdims=False)
        source = jnp.where(sector_index == 0, initial, incoming).astype(jnp.float32)
        wavenumber = jnp.sqrt(energies[energy_slot] - channel_thresholds)[:, None]
        values_part = source[:, 0, :]
        slopes_part = source[:, 1, :]
        cosine = jnp.cos(wavenumber)
        sine_term = jnp.sin(wavenumber)
        new_values = cosine * values_part + sine_term / wavenumber * slopes_part
        new_slopes = -wavenumber * sine_term * values_part + cosine * slopes_part
        rotated = jnp.stack([new_values, new_slopes], axis=1).astype(jnp.bfloat16)
        flat = rotated.reshape(channel_count, 2 * col_width)
        fresh = lax.cond(active, multiply, skipped, flat)
        fresh = fresh.reshape(channel_count, 2, col_width)
        previous = lax.dynamic_index_in_dim(stored, energy_slot, 0, keepdims=False)
        kept = jnp.where(active, fresh, previous)
        stored = lax.dynamic_update_index_in_dim(stored, kept, energy_slot, 0)
        return (fresh, stored)

    outgoing_init = jnp.zeros((channel_count, 2, col_width), jnp.bfloat16)
    final_pair = lax.fori_loop(0, step_count, step, (outgoing_init, stored_init))
    returned = lax.all_to_all(final_pair[1], "ch", split_axis=1, concat_axis=3, tiled=True)
    return returned.reshape(energy_count, row_count, width_cols)[None]


AUX_ROWS = 16
ROTATE_ROWS = 64


def sweep_kernel(
    sectors, groups, start, levels, own_block, out,
    basis, amps, rotated, kept, turn,
    local_sem, block_recv, spread_send, up_send, down_send, core_send,
    start_recv, start_up, start_down, out_send, out_recv, out_local,
):
    k = lax.axis_index("sec")
    z = lax.axis_index("ch")
    core = k % 2
    partner = k + 1 - 2 * core
    pairs = sectors // 2
    energy_count, row_count, width_cols = start.shape
    half_cols = width_cols // 2
    width = half_cols // sectors
    channel_count = row_count * groups
    has_up = z + 1 < groups
    has_down = z >= 1

    def remote(src, dst, send, recv, **where):
        return pltpu.make_async_remote_copy(
            src_ref=src, dst_ref=dst, send_sem=send, recv_sem=recv,
            device_id=where, device_id_type=pl.DeviceIdType.MESH,
        )

    def rows_of(c):
        return pl.ds(pl.multiple_of(c * row_count, row_count), row_count)

    def block_up(i, c):
        s = 2 * i + core
        return remote(basis.at[s, c], basis.at[s, c], up_send.at[i, c], block_recv.at[s, c], ch=z + 1)

    def block_down(i, c):
        s = 2 * i + core
        return remote(basis.at[s, c], basis.at[s, c], down_send.at[i, c], block_recv.at[s, c], ch=z - 1)

    def block_core(i, c):
        s = 2 * i + core
        return remote(basis.at[s, c], basis.at[s, c], core_send.at[i, c], block_recv.at[s, c], sec=partner)

    def block_spread(step):
        target = 2 * ((k // 2 + step) % pairs) + core
        return remote(basis.at[k, z], basis.at[k, z], spread_send.at[step], block_recv.at[k, z], sec=target)

    def block_arrived(s, c):
        remote(basis.at[s, c], basis.at[s, c], core_send.at[0, 0], block_recv.at[s, c], sec=partner).wait_recv()

    def start_part(e, c):
        return amps.at[0, e, rows_of(c), :]

    def start_move(e, c, send, **where):
        return remote(start_part(e, c), start_part(e, c), send.at[c], start_recv.at[e, c], **where)

    def start_arrived(e, c):
        remote(start_part(e, c), start_part(e, c), start_up.at[0], start_recv.at[e, c], sec=partner).wait_recv()

    loads = [
        pltpu.make_async_copy(own_block, basis.at[k, z], local_sem.at[0]),
        pltpu.make_async_copy(
            start.at[:, :, pl.ds(pl.multiple_of(k * width, width), width)],
            amps.at[0, :, rows_of(z), pl.ds(0, width)], local_sem.at[1]),
        pltpu.make_async_copy(
            start.at[:, :, pl.ds(pl.multiple_of(half_cols + k * width, width), width)],
            amps.at[0, :, rows_of(z), pl.ds(width, width)], local_sem.at[2]),
    ]
    for load in loads:
        load.start()

    barrier = pltpu.get_barrier_semaphore()
    for step in range(1, sectors):
        pl.semaphore_signal(barrier, inc=1, device_id={"sec": (k + step) % sectors}, device_id_type=pl.DeviceIdType.MESH)

    @pl.when(has_up)
    def _():
        pl.semaphore_signal(barrier, inc=1, device_id={"ch": z + 1}, device_id_type=pl.DeviceIdType.MESH)

    @pl.when(has_down)
    def _():
        pl.semaphore_signal(barrier, inc=1, device_id={"ch": z - 1}, device_id_type=pl.DeviceIdType.MESH)

    line_peers = jnp.minimum(z, 1) + jnp.minimum(groups - 1 - z, 1)
    pl.semaphore_wait(barrier, sectors - 1 + line_peers)
    for load in loads:
        load.wait()
    for step in range(1, pairs):
        block_spread(step).start()

    def each_energy(action):
        @pl.loop(0, energy_count)
        def _(e):
            action(e)

    @pl.when(has_up)
    def _():
        each_energy(lambda e: start_move(e, z, start_up, ch=z + 1).start())

    @pl.when(has_down)
    def _():
        each_energy(lambda e: start_move(e, z, start_down, ch=z - 1).start())

    def own_step(i):
        s = 2 * i + core

        @pl.when(s != k)
        def _():
            block_arrived(s, z)

        @pl.when(has_up)
        def _():
            block_up(i, z).start()

        @pl.when(has_down)
        def _():
            block_down(i, z).start()

        block_core(i, z).start()

    def forward_step(i, d):
        s = 2 * i + core

        @pl.when(z - d >= 0)
        def _():
            block_arrived(s, z - d)

            @pl.when(has_up)
            def _():
                block_up(i, z - d).start()

            block_core(i, z - d).start()

        @pl.when(z + d < groups)
        def _():
            block_arrived(s, z + d)

            @pl.when(has_down)
            def _():
                block_down(i, z + d).start()

            block_core(i, z + d).start()

    def start_forward(d):
        @pl.when(z - d >= 0)
        def _():
            def action(e):
                start_arrived(e, z - d)

                @pl.when(has_up)
                def _():
                    start_move(e, z - d, start_up, ch=z + 1).start()

            each_energy(action)

        @pl.when(z + d < groups)
        def _():
            def action(e):
                start_arrived(e, z + d)

                @pl.when(has_down)
                def _():
                    start_move(e, z + d, start_down, ch=z - 1).start()

            each_energy(action)

    lag = max(groups // 2, 1)
    own_step(0)
    for d in range(1, groups):
        start_forward(d)
        forward_step(0, d)
        if pairs > 1 and d == lag:
            own_step(1)
        if pairs > 1 and d > lag:
            forward_step(1, d - lag)

    def send_energy(s, e):
        for half in range(2):
            columns = pl.ds(pl.multiple_of(half * half_cols + k * width, width), width)

            @pl.when(s == k)
            def _():
                pltpu.make_async_copy(kept.at[s, half, e], out.at[e, :, columns], out_local.at[0]).start()

            @pl.when(s != k)
            def _():
                remote(kept.at[s, half, e], out.at[e, :, columns], out_send.at[s], out_recv.at[k], sec=s).start()

    def rotate(s):
        source = jnp.minimum(s, 1)

        @pl.loop(0, groups)
        def _(c):
            limits = basis[s, c, row_count:, :row_count].astype(jnp.float32)[0:1, :]
            wavenumber = jnp.sqrt(levels[...][:, 0:1] - limits)
            cosine = jnp.cos(wavenumber)
            sine_term = jnp.sin(wavenumber)
            rows = wavenumber.shape[0]
            filler = jnp.zeros((128 - 3 * rows, row_count), jnp.float32)
            stacked = jnp.concatenate(
                [cosine, sine_term / wavenumber, -wavenumber * sine_term, filler], axis=0
            )
            turn[...] = stacked.T

            @pl.loop(0, row_count // ROTATE_ROWS)
            def _(r):
                local = pl.ds(pl.multiple_of(r * ROTATE_ROWS, ROTATE_ROWS), ROTATE_ROWS)
                place = pl.ds(pl.multiple_of(c * row_count + r * ROTATE_ROWS, ROTATE_ROWS), ROTATE_ROWS)
                factors = turn[local, :]
                for e in range(energy_count):
                    both = amps[source, e, place, :].astype(jnp.float32)
                    values_part, slopes_part = both[:, :width], both[:, width:]
                    keep = factors[:, e : e + 1]
                    rise = factors[:, rows + e : rows + e + 1]
                    fall = factors[:, 2 * rows + e : 2 * rows + e + 1]
                    rotated[e, place, pl.ds(0, width)] = (keep * values_part + rise * slopes_part).astype(jnp.bfloat16)
                    rotated[e, place, pl.ds(width, width)] = (fall * values_part + keep * slopes_part).astype(jnp.bfloat16)

    def multiply(s):
        @pl.loop(0, energy_count)
        def _(e):
            @pl.loop(0, groups)
            def _(c):
                @pl.when((s < sectors - 1) | (c == z))
                def _():
                    product = jnp.dot(
                        basis[s, c, :row_count, :], rotated[e], preferred_element_type=jnp.float32
                    ).astype(jnp.bfloat16)
                    amps[1, e, rows_of(c), :] = product

                    @pl.when(c == z)
                    def _():
                        kept[s, 0, e] = product[:, :width]
                        kept[s, 1, e] = product[:, width:]

            @pl.when(e >= 1)
            def _():
                send_energy(s, e - 1)

    @pl.loop(0, pairs)
    def _(i):
        more = i + 1 < pairs
        further = i + 2 < pairs

        @pl.when(further)
        def _():
            own_step(i + 2)

        for c in range(groups):
            block_arrived(2 * i + 1 - core, c)
        rotate(2 * i)

        @pl.when(i >= 1)
        def _():
            send_energy(2 * i - 1, energy_count - 1)

        multiply(2 * i)

        @pl.when(more)
        def _():
            for d in range(max(groups - lag, 1), groups - 1):
                forward_step(i + 1, d)

        rotate(2 * i + 1)
        send_energy(2 * i, energy_count - 1)
        multiply(2 * i + 1)

        @pl.when(more)
        def _():
            forward_step(i + 1, groups - 1)

        @pl.when(further)
        def _():
            for d in range(1, groups - lag):
                forward_step(i + 2, d)

    for step in range(1, pairs):
        block_spread(step).wait_send()

    @pl.loop(0, pairs)
    def _(i):
        for c in range(groups):
            block_core(i, c).wait_send()

            @pl.when(has_up & (c <= z))
            def _():
                block_up(i, c).wait_send()

            @pl.when(has_down & (c >= z))
            def _():
                block_down(i, c).wait_send()

    for c in range(groups):
        span = amps.at[0, :, pl.ds(c * row_count, row_count), :]

        @pl.when(has_up & (c <= z))
        def _():
            remote(span, span, start_up.at[c], start_recv.at[0, 0], ch=z + 1).wait_send()

        @pl.when(has_down & (c >= z))
        def _():
            remote(span, span, start_down.at[c], start_recv.at[0, 0], ch=z - 1).wait_send()

    send_energy(sectors - 1, energy_count - 1)

    @pl.loop(0, sectors)
    def _(s):
        whole = remote(kept.at[s], kept.at[s], out_send.at[s], out_recv.at[s], sec=partner)

        @pl.when(s != k)
        def _():
            whole.wait_send()
            whole.wait_recv()

        @pl.when(s == k)
        def _():
            pltpu.make_async_copy(kept.at[s], kept.at[s], out_local.at[0]).wait()


def per_device_swept(start_amps, energies, thresholds, intersection):
    sectors = lax.axis_size("sec")
    groups = lax.axis_size("ch")
    energy_count, row_count, width_cols = start_amps.shape
    channel_count = intersection.shape[2]
    width = width_cols // 2 // sectors
    pairs = sectors // 2
    padded = jnp.concatenate([energies, jnp.broadcast_to(energies[:1], (-energy_count % 8,))])
    levels = jnp.broadcast_to(padded[:, None], (padded.shape[0], 128))
    aux = jnp.pad(thresholds, ((0, AUX_ROWS - 1), (0, channel_count - row_count)))
    own_block = jnp.concatenate([intersection[0], aux], axis=0)
    dma = pltpu.SemaphoreType.DMA
    stored = jax.ShapeDtypeStruct(start_amps.shape, jnp.bfloat16)
    swept = pl.pallas_call(
        functools.partial(sweep_kernel, sectors, groups),
        out_shape=stored,
        in_specs=[
            pl.BlockSpec(memory_space=pl.ANY),
            pl.BlockSpec(memory_space=pltpu.VMEM),
            pl.BlockSpec(memory_space=pl.ANY),
        ],
        out_specs=pl.BlockSpec(memory_space=pl.ANY),
        scratch_shapes=[
            pltpu.VMEM((sectors, groups, row_count + AUX_ROWS, channel_count), jnp.bfloat16),
            pltpu.VMEM((2, energy_count, channel_count, 2 * width), jnp.bfloat16),
            pltpu.VMEM((energy_count, channel_count, 2 * width), jnp.bfloat16),
            pltpu.VMEM((sectors, 2, energy_count, row_count, width), jnp.bfloat16),
            pltpu.VMEM((row_count, 128), jnp.float32),
            dma((3,)),
            dma((sectors, groups)),
            dma((pairs,)),
            dma((pairs, groups)),
            dma((pairs, groups)),
            dma((pairs, groups)),
            dma((energy_count, groups)),
            dma((groups,)),
            dma((groups,)),
            dma((sectors,)),
            dma((sectors,)),
            dma((1,)),
        ],
        compiler_params=pltpu.CompilerParams(
            collective_id=0, has_side_effects=True, vmem_limit_bytes=60 * 2**20
        ),
    )(start_amps, levels, own_block)
    return swept[None]


GATHERED_LIMIT = 24 * 2**20


def per_device(start_amps, energies, thresholds, intersection):
    sectors = lax.axis_size("sec")
    row_count, channel_count = intersection.shape[1:]
    gathered_bytes = sectors * channel_count**2 * intersection.dtype.itemsize
    even = sectors % 2 == 0 and (start_amps.shape[2] // 2) % (sectors * 128) == 0
    even = even and row_count % 128 == 0 and energies.shape[0] <= 40
    if even and gathered_bytes <= GATHERED_LIMIT:
        return per_device_swept(start_amps, energies, thresholds, intersection)
    return per_device_pipelined(start_amps, energies, thresholds, intersection)


def solution(mesh):
    in_specs = (P(None, "ch", None), P(), P("sec", "ch"), P("sec", "ch", None))
    out_specs = P("sec", None, "ch", None)
    return jax.shard_map(
        per_device, mesh=mesh, in_specs=in_specs, out_specs=out_specs, check_vma=False
    )
```

profile of v0, /device:TPU:7, one launch (start us, length us, event | category | flops | bytes accessed | tf_op | source)
XLA Modules:
  0.0 291.0 jit_solution(6475032391501084918)
XLA Ops:
  0.0 1.3 concatenate.6
  1.3 0.7 broadcast_in_dim.7.levels
  2.0 1.9 fusion.1.own_block
  3.9 280.5 %shard_map.46 = bf16[6,256,2048]{2,1,0:T(8,128)(2,1)} custom-call(bf16[6,256,2048]{2,1,0:T(8,128)(2,1)} %start.1, f32[8,128]{1,0:T(8,128)} %broadcast_in_dim.7.levels, bf16[272,1024]{1,0:T(8,128)(2,1)} %fusion.1.own_block), custom_call_target="tpu_custom_call" | custom-call | tf_op jit(solution)/shard_map/pallas_call | solution.py:405
  284.3 6.6 %copy.6 = bf16[1,6,256,2048]{3,2,1,0:T(8,128)(2,1)} copy(bf16[1,6,256,2048]{3,2,1,0:T(8,128)(2,1)} %bitcast.4) | data formatting | bytes 12582912
where the time goes:
time: 291 us
  Pallas kernels  280 us (96%)
  local copies, waits for them, and re-layouts  8.58 us (3%)
    pallas_call x1, Pallas kernels, per_device_swept(): pl.pallas_call(functools.partial(sweep_kernel, sectors, groups), out_shap...  280 us
    unnamed x1, local copies, waits for them, and re-layouts  6.61 us

commit v1 on v0

v1 whole, which is shorter than its diff:
```python
import functools
import jax
import jax.numpy as jnp
from jax import lax
from jax.experimental import pallas as pl
from jax.experimental.pallas import tpu as pltpu
from jax.sharding import PartitionSpec as P


def passed_along(value, axis, steps):
    count = lax.axis_size(axis)
    leading, last = (max(0, -steps), min(count, count - steps))
    return lax.ppermute(value, axis, [(source, source + steps) for source in range(leading, last)])


def per_device_pipelined(start_amps, energies, thresholds, intersection):
    sectors = lax.axis_size("sec")
    sector_index = lax.axis_index("sec")
    groups = lax.axis_size("ch")
    energy_count = energies.shape[0]
    step_count = sectors + energy_count - 1
    row_count = intersection.shape[1]
    width_cols = start_amps.shape[2]
    half_cols = width_cols // 2
    col_width = half_cols // groups
    intersection_whole, thresholds_whole = (
        lax.all_gather(intersection, "ch", axis=1, tiled=True),
        lax.all_gather(thresholds, "ch", axis=1, tiled=True),
    )
    basis_change = intersection_whole[0]
    channel_thresholds = thresholds_whole[0].astype(jnp.float32)
    channel_count = basis_change.shape[0]
    paired = start_amps.reshape(energy_count, row_count, 2, half_cols)
    start_cols = lax.all_to_all(paired, "ch", split_axis=3, concat_axis=1, tiled=True)
    stored_init = jnp.zeros((energy_count, channel_count, 2, col_width), jnp.bfloat16)

    def multiply(flat):
        return jnp.dot(basis_change, flat, preferred_element_type=jnp.float32).astype(jnp.bfloat16)

    def skipped(flat):
        return jnp.zeros((channel_count, 2 * col_width), jnp.bfloat16)

    def step(step_index, state_pair):
        outgoing, stored = state_pair
        incoming = passed_along(outgoing, "sec", 1)
        energy_raw = step_index - sector_index
        active = (energy_raw >= 0) & (energy_raw < energy_count)
        energy_slot = jnp.clip(energy_raw, 0, energy_count - 1)
        initial = lax.dynamic_index_in_dim(start_cols, energy_slot, 0, keepdims=False)
        source = jnp.where(sector_index == 0, initial, incoming).astype(jnp.float32)
        wavenumber = jnp.sqrt(energies[energy_slot] - channel_thresholds)[:, None]
        values_part = source[:, 0, :]
        slopes_part = source[:, 1, :]
        cosine = jnp.cos(wavenumber)
        sine_term = jnp.sin(wavenumber)
        new_values = cosine * values_part + sine_term / wavenumber * slopes_part
        new_slopes = -wavenumber * sine_term * values_part + cosine * slopes_part
        rotated = jnp.stack([new_values, new_slopes], axis=1).astype(jnp.bfloat16)
        flat = rotated.reshape(channel_count, 2 * col_width)
        fresh = lax.cond(active, multiply, skipped, flat)
        fresh = fresh.reshape(channel_count, 2, col_width)
        previous = lax.dynamic_index_in_dim(stored, energy_slot, 0, keepdims=False)
        kept = jnp.where(active, fresh, previous)
        stored = lax.dynamic_update_index_in_dim(stored, kept, energy_slot, 0)
        return (fresh, stored)

    outgoing_init = jnp.zeros((channel_count, 2, col_width), jnp.bfloat16)
    final_pair = lax.fori_loop(0, step_count, step, (outgoing_init, stored_init))
    returned = lax.all_to_all(final_pair[1], "ch", split_axis=1, concat_axis=3, tiled=True)
    return returned.reshape(energy_count, row_count, width_cols)[None]


LANES = 128
STAGES = 5


def sweep_kernel(
    sectors, groups, start, energies, limits, own_block, out,
    basis, amps, rotated, kept, turn, bounds,
    local_sem, block_recv, side_send, over_send, up_send, down_send, core_send,
    start_recv, start_up, start_down, bound_send, bound_recv, out_send, out_recv, out_local,
):
    k = lax.axis_index("sec")
    z = lax.axis_index("ch")
    core = k % 2
    chip = k // 2
    column, row = chip % 2, chip // 2
    partner = k + 1 - 2 * core
    column_peer = k + 2 - 4 * column
    row_peer = k + 4 - 8 * row
    pairs = sectors // 2
    last = sectors - 1
    energy_count, row_count, width_cols = start.shape
    half_cols = width_cols // 2
    width = half_cols // sectors
    channel_count = row_count * groups
    chunks = channel_count // LANES
    devices = sectors * groups
    has_up = z + 1 < groups
    has_down = z >= 1
    rounds = max(pairs, energy_count)
    inputs = 2 * rounds

    def remote(src, dst, send, recv, **where):
        return pltpu.make_async_remote_copy(
            src_ref=src, dst_ref=dst, send_sem=send, recv_sem=recv,
            device_id=where, device_id_type=pl.DeviceIdType.MESH,
        )

    def rows_of(c):
        return pl.ds(pl.multiple_of(c * row_count, row_count), row_count)

    def other(step):
        place = (k * groups + z + step) % devices
        return {"sec": place // groups, "ch": place % groups}

    def block_move(s, b, send, **where):
        part = basis.at[s, rows_of(b), :]
        return remote(part, part, send.at[s // 2, b], block_recv.at[s, b], **where)

    def routes(pair, b):
        s = 2 * pair + core
        across = pair % 2
        near = jnp.where(across == 0, row == pair // 2, column == pair % 2)
        carrier = near != (core == 1)
        home = b == z
        along = (s < last) & carrier
        return s, [
            (along & has_up & (b <= z), lambda: block_move(s, b, up_send, ch=z + 1)),
            (along & has_down & (b >= z), lambda: block_move(s, b, down_send, ch=z - 1)),
            (home & (chip == pair), lambda: block_move(s, b, side_send, sec=jnp.where(across == 0, column_peer, row_peer))),
            (jnp.where(home, near, carrier), lambda: block_move(s, b, over_send, sec=jnp.where(across == 0, row_peer, column_peer))),
            (b >= 0, lambda: block_move(s, b, core_send, sec=partner)),
        ]

    def travels(s, b):
        return (s < last) | (b == z)

    def relay(pair, b):
        for wanted, move in routes(pair, b)[1]:
            @pl.when(wanted)
            def _():
                move().start()

    def block_arrived(s, b):
        block_move(s, b, core_send, sec=partner).wait_recv()

    def arrive_and_relay(pair, b):
        s = 2 * pair + core

        @pl.when((b >= 0) & (b < groups) & travels(s, b))
        def _():
            block_arrived(s, b)
            relay(pair, b)

    def start_part(e, c):
        return amps.at[0, e, rows_of(c), :]

    def start_move(e, c, send, **where):
        return remote(start_part(e, c), start_part(e, c), send.at[c], start_recv.at[e, c], **where)

    def start_relay(e, c):
        @pl.when(has_up & (c <= z))
        def _():
            start_move(e, c, start_up, ch=z + 1).start()

        @pl.when(has_down & (c >= z))
        def _():
            start_move(e, c, start_down, ch=z - 1).start()

    def start_arrive_and_relay(e, c):
        @pl.when((c >= 0) & (c < groups))
        def _():
            start_move(e, c, start_up, sec=partner).wait_recv()
            start_relay(e, c)

    def event(item, stage):
        own = (stage == 0) & (item + 2 < inputs)
        passed = (stage == 1) & (item + 1 < inputs)
        hop = stage - 1
        ahead = item + jnp.where(stage == 0, 2, jnp.where(stage == 1, 1, 0))
        place = ahead // 2
        is_pair = (ahead % 2 == 0) & (place < pairs)
        is_start = (ahead % 2 == 1) & (place < energy_count)

        @pl.when(is_pair & own & (chip == place))
        def _():
            relay(place, z)

        @pl.when(is_pair & passed & (chip != place))
        def _():
            arrive_and_relay(place, z)

        @pl.when(is_pair & (stage >= 2))
        def _():
            @pl.loop(0, 2)
            def _(side):
                arrive_and_relay(place, z - hop + 2 * hop * side)

        @pl.when(is_start & own)
        def _():
            start_relay(place, z)

        @pl.when(is_start & (stage >= 2))
        def _():
            @pl.loop(0, 2)
            def _(side):
                start_arrive_and_relay(place, z - hop + 2 * hop * side)

    loads = [
        pltpu.make_async_copy(own_block, basis.at[k, rows_of(z), :], local_sem.at[0]),
        pltpu.make_async_copy(
            start.at[:, :, pl.ds(pl.multiple_of(k * width, width), width)],
            amps.at[0, :, rows_of(z), pl.ds(0, width)], local_sem.at[1]),
        pltpu.make_async_copy(
            start.at[:, :, pl.ds(pl.multiple_of(half_cols + k * width, width), width)],
            amps.at[0, :, rows_of(z), pl.ds(width, width)], local_sem.at[2]),
        pltpu.make_async_copy(limits, bounds.at[k, z], local_sem.at[3]),
    ]
    for load in loads:
        load.start()

    barrier = pltpu.get_barrier_semaphore()

    @pl.loop(1, devices)
    def _(step):
        pl.semaphore_signal(barrier, inc=1, device_id=other(step), device_id_type=pl.DeviceIdType.MESH)

    pl.semaphore_wait(barrier, devices - 1)
    loads[0].wait()

    @pl.when(chip == 0)
    def _():
        relay(0, z)

    for load in loads[1:]:
        load.wait()

    def bound_move(step):
        return pltpu.make_async_remote_copy(
            src_ref=bounds.at[k, z], dst_ref=bounds.at[k, z], send_sem=bound_send.at[step], recv_sem=bound_recv.at[k, z],
            device_id=other(step), device_id_type=pl.DeviceIdType.MESH,
        )

    @pl.loop(1, devices)
    def _(step):
        bound_move(step).start()

    start_relay(0, z)

    @pl.when(chip != 0)
    def _():
        arrive_and_relay(0, z)

    @pl.loop(0, sectors)
    def _(s):
        for c in range(groups):
            @pl.when((s != k) | (c != z))
            def _():
                remote(bounds.at[s, c], bounds.at[s, c], bound_send.at[0], bound_recv.at[s, c], sec=partner).wait_recv()

        floor = jnp.concatenate([bounds[s, c] for c in range(groups)], axis=0)
        for e in range(energy_count):
            wavenumber = jnp.sqrt(energies[e] - floor)
            cosine = jnp.cos(wavenumber)
            sine_term = jnp.sin(wavenumber)
            filler = jnp.zeros((LANES - 3 * chunks, LANES), jnp.float32)
            stacked = jnp.concatenate(
                [cosine, sine_term / wavenumber, -wavenumber * sine_term, filler], axis=0
            )
            turn[s, e] = stacked.T

    def advance(s, e):
        source = jnp.minimum(s, 1)
        factors = turn[s, e]
        for q in range(chunks):
            place = pl.ds(q * LANES, LANES)
            both = amps[source, e, place, :].astype(jnp.float32)
            values_part, slopes_part = both[:, :width], both[:, width:]
            keep = factors[:, q : q + 1]
            rise = factors[:, chunks + q : chunks + q + 1]
            fall = factors[:, 2 * chunks + q : 2 * chunks + q + 1]
            rotated[place, pl.ds(0, width)] = (keep * values_part + rise * slopes_part).astype(jnp.bfloat16)
            rotated[place, pl.ds(width, width)] = (fall * values_part + keep * slopes_part).astype(jnp.bfloat16)

        @pl.when(s < last)
        def _():
            amps[1, e] = jnp.dot(basis[s], rotated[...], preferred_element_type=jnp.float32).astype(jnp.bfloat16)
            mine = amps[1, e, rows_of(z), :]
            kept[s, 0, e] = mine[:, :width]
            kept[s, 1, e] = mine[:, width:]

        @pl.when(s == last)
        def _():
            mine = jnp.dot(
                basis[s, rows_of(z), :], rotated[...], preferred_element_type=jnp.float32
            ).astype(jnp.bfloat16)
            kept[s, 0, e] = mine[:, :width]
            kept[s, 1, e] = mine[:, width:]

    def send_out(s, e):
        for half in range(2):
            columns = pl.ds(pl.multiple_of(half * half_cols + k * width, width), width)

            @pl.when(s == k)
            def _():
                pltpu.make_async_copy(kept.at[s, half, e], out.at[e, :, columns], out_local.at[0]).start()

            @pl.when(s != k)
            def _():
                remote(kept.at[s, half, e], out.at[e, :, columns], out_send.at[s], out_recv.at[k], sec=s).start()

    @pl.loop(0, inputs + 1)
    def _(upcoming):
        done = upcoming - 1
        place = jnp.maximum(done, 0) // 2
        from_pair = done % 2 == 0
        ready = jnp.minimum(2 * place + 2, sectors)
        pair_steps = jnp.where(place < pairs, 2 * jnp.minimum(place, energy_count), 0)
        start_steps = jnp.where(place < energy_count, ready, 0)
        steps = jnp.where(done < 0, 0, jnp.where(from_pair, pair_steps, start_steps))

        def task(i):
            return (
                jnp.where(from_pair, 2 * place + i % 2, i),
                jnp.where(from_pair, i // 2, place),
            )

        @pl.loop(0, jnp.maximum(steps + 1, STAGES))
        def _(i):
            @pl.when(i < steps)
            def _():
                advance(*task(i))

            @pl.when((i >= 1) & (i <= steps))
            def _():
                send_out(*task(i - 1))

            @pl.when((i < STAGES) & (upcoming < inputs))
            def _():
                event(upcoming, i)

        @pl.when((upcoming % 2 == 0) & (upcoming // 2 < pairs))
        def _():
            s = 2 * (upcoming // 2) + 1 - core
            for b in range(groups):
                @pl.when(travels(s, b))
                def _():
                    block_arrived(s, b)

    @pl.loop(1, devices)
    def _(step):
        bound_move(step).wait_send()

    @pl.loop(0, pairs)
    def _(pair):
        for b in range(groups):
            s, moves = routes(pair, b)

            @pl.when(travels(s, b))
            def _():
                for wanted, move in moves:
                    @pl.when(wanted)
                    def _():
                        move().wait_send()

    for c in range(groups):
        span = amps.at[0, :, pl.ds(c * row_count, row_count), :]

        @pl.when(has_up & (c <= z))
        def _():
            remote(span, span, start_up.at[c], start_recv.at[0, 0], ch=z + 1).wait_send()

        @pl.when(has_down & (c >= z))
        def _():
            remote(span, span, start_down.at[c], start_recv.at[0, 0], ch=z - 1).wait_send()

    @pl.loop(0, sectors)
    def _(s):
        whole = remote(kept.at[s], kept.at[s], out_send.at[s], out_recv.at[s], sec=partner)

        @pl.when(s != k)
        def _():
            whole.wait_send()
            whole.wait_recv()

        @pl.when(s == k)
        def _():
            pltpu.make_async_copy(kept.at[s], kept.at[s], out_local.at[0]).wait()


def per_device_swept(start_amps, energies, thresholds, intersection):
    sectors = lax.axis_size("sec")
    groups = lax.axis_size("ch")
    energy_count, row_count, width_cols = start_amps.shape
    channel_count = intersection.shape[2]
    width = width_cols // 2 // sectors
    pairs = sectors // 2
    limits = thresholds.reshape(row_count // LANES, LANES).astype(jnp.float32)
    dma = pltpu.SemaphoreType.DMA
    stored = jax.ShapeDtypeStruct(start_amps.shape, jnp.bfloat16)
    swept = pl.pallas_call(
        functools.partial(sweep_kernel, sectors, groups),
        out_shape=stored,
        in_specs=[
            pl.BlockSpec(memory_space=pl.ANY),
            pl.BlockSpec(memory_space=pltpu.SMEM),
            pl.BlockSpec(memory_space=pl.ANY),
            pl.BlockSpec(memory_space=pl.ANY),
        ],
        out_specs=pl.BlockSpec(memory_space=pl.ANY),
        scratch_shapes=[
            pltpu.VMEM((sectors, channel_count, channel_count), jnp.bfloat16),
            pltpu.VMEM((2, energy_count, channel_count, 2 * width), jnp.bfloat16),
            pltpu.VMEM((channel_count, 2 * width), jnp.bfloat16),
            pltpu.VMEM((sectors, 2, energy_count, row_count, width), jnp.bfloat16),
            pltpu.VMEM((sectors, energy_count, LANES, LANES), jnp.float32),
            pltpu.VMEM((sectors, groups, row_count // LANES, LANES), jnp.float32),
            dma((4,)),
            dma((sectors, groups)),
            dma((pairs, groups)),
            dma((pairs, groups)),
            dma((pairs, groups)),
            dma((pairs, groups)),
            dma((pairs, groups)),
            dma((energy_count, groups)),
            dma((groups,)),
            dma((groups,)),
            dma((sectors * groups,)),
            dma((sectors, groups)),
            dma((sectors,)),
            dma((sectors,)),
            dma((1,)),
        ],
        compiler_params=pltpu.CompilerParams(
            collective_id=0, has_side_effects=True, vmem_limit_bytes=60 * 2**20
        ),
    )(start_amps, energies, limits, intersection[0])
    return swept[None]


GATHERED_LIMIT = 24 * 2**20


def per_device(start_amps, energies, thresholds, intersection):
    sectors = lax.axis_size("sec")
    row_count, channel_count = intersection.shape[1:]
    gathered_bytes = sectors * channel_count**2 * intersection.dtype.itemsize
    even = sectors // 2 == 4 and (start_amps.shape[2] // 2) % (sectors * LANES) == 0
    even = even and row_count % LANES == 0 and 3 * (channel_count // LANES) <= LANES
    if even and gathered_bytes <= GATHERED_LIMIT:
        return per_device_swept(start_amps, energies, thresholds, intersection)
    return per_device_pipelined(start_amps, energies, thresholds, intersection)


def solution(mesh):
    in_specs = (P(None, "ch", None), P(), P("sec", "ch"), P("sec", "ch", None))
    out_specs = P("sec", None, "ch", None)
    return jax.shard_map(
        per_device, mesh=mesh, in_specs=in_specs, out_specs=out_specs, check_vma=False
    )
```

time: 291 us -> 310 us (1.065)
  Pallas kernels: 280 us -> 301 us
    pallas_call x1, Pallas kernels: 280 us -> 301 us  [per_device_swept(): pl.pallas_call(functools.partial(sweep_kernel, sectors, groups), out_shap...]
where the time goes in v1:
time: 310 us; the launch traced here: 309 us
  Pallas kernels  301 us (97%)
  local copies, waits for them, and re-layouts  6.61 us (2%)
    pallas_call x1, Pallas kernels, per_device_swept(): pl.pallas_call(functools.partial(sweep_kernel, sectors, groups), out_shap...  301 us
    unnamed x1, local copies, waits for them, and re-layouts  6.61 us

profile of v1, /device:TPU:7, one launch (start us, length us, event | category | flops | bytes accessed | tf_op | source)
XLA Modules:
  0.0 309.0 jit_solution(15301367880051899110)
XLA Ops:
  0.0 1.2 convert_element_type.7
  1.2 301.2 %shard_map.46 = bf16[6,256,2048]{2,1,0:T(8,128)(2,1)} custom-call(bf16[6,256,2048]{2,1,0:T(8,128)(2,1)} %start.1, f32[6]{0:T(128)} %energies.1, f32[2,128]{1,0:T(2,128)} %bitcast.5, bf16[256,1024]{1,0:T(8,128)(2,1)} %bitcast.4), custom_call_target="tpu_custom_call" | custom-call | tf_op jit(solution)/shard_map/pallas_call | solution.py:402
  302.4 6.6 %copy.6 = bf16[1,6,256,2048]{3,2,1,0:T(8,128)(2,1)} copy(bf16[1,6,256,2048]{3,2,1,0:T(8,128)(2,1)} %bitcast.3) | data formatting | bytes 12582912

commit v2 on v1

--- a/solution.py
+++ b/solution.py
@@ -71,13 +71,55 @@
 
 
 LANES = 128
-STAGES = 5
+HOME, LIFT, HOP, SIDE, TWIN, FEED, FEED_HOP, STEP, ANGLES, END = range(10)
+TUNED = (
+    (5, 0, 0), (5, 1, 0), (6, 0, 1), (6, 0, 2), (0, 0, 0), (1, 0, 0), (2, 0, 1), (3, 0, 1), (0, 1, 0), (2, 0, 2),
+    (1, 1, 0), (3, 0, 2), (2, 0, 3), (2, 1, 1), (0, 3, 0), (1, 3, 0), (2, 1, 2), (0, 2, 0), (2, 1, 3), (3, 1, 2),
+    (1, 2, 0), (3, 0, 3), (4, 0, 0), (3, 1, 1), (2, 2, 1), (2, 3, 1), (3, 1, 3), (2, 2, 2), (2, 3, 2), (3, 2, 1),
+    (3, 3, 1), (4, 1, 0), (6, 0, 3), (3, 2, 2), (2, 2, 3), (7, 0, 0), (2, 3, 3), (3, 2, 3), (3, 3, 2), (3, 3, 3),
+    (6, 1, 1), (5, 2, 0), (7, 1, 0), (7, 2, 0), (4, 2, 0), (6, 1, 2), (5, 3, 0), (7, 3, 0), (7, 4, 0), (6, 2, 1),
+    (7, 5, 0), (4, 3, 0), (7, 6, 0), (6, 1, 3), (7, 0, 1), (7, 7, 0), (7, 1, 1), (7, 2, 1), (6, 3, 1), (7, 3, 1),
+    (7, 4, 1), (6, 2, 2), (7, 5, 1), (6, 2, 3), (5, 4, 0), (6, 3, 2), (7, 6, 1), (7, 0, 2), (7, 7, 1), (5, 5, 0),
+    (7, 1, 2), (7, 2, 2), (6, 3, 3), (7, 3, 2), (7, 4, 2), (7, 0, 3), (6, 5, 1), (7, 1, 3), (6, 4, 1), (7, 5, 2),
+    (7, 6, 2), (6, 5, 2), (7, 2, 3), (7, 7, 2), (7, 3, 3), (7, 4, 3), (7, 5, 3), (7, 6, 3), (6, 4, 2), (6, 5, 3),
+    (7, 0, 5), (7, 1, 5), (6, 4, 3), (7, 7, 3), (7, 0, 4), (7, 2, 5), (7, 3, 5), (7, 1, 4), (7, 2, 4), (7, 4, 5),
+    (7, 5, 5), (7, 3, 4), (7, 4, 4), (7, 6, 5), (7, 5, 4), (7, 7, 5), (7, 6, 4), (7, 7, 4),
+)
+
+
+def plain_order(pairs, sectors, energy_count, groups):
+    order = [(HOME, j, 0) for j in range(pairs)]
+    order += [(FEED, e, 0) for e in range(energy_count)] + [(LIFT, j, 0) for j in range(pairs)]
+    for tick in range(pairs + groups):
+        for d in range(groups - 1, 0, -1):
+            if 0 <= tick - d < pairs:
+                order.append((HOP, tick - d, d))
+            if 0 <= tick - d - 1 < pairs:
+                order.append((SIDE, tick - d - 1, d))
+    order += [(TWIN, j, 0) for j in range(pairs)]
+    for e in range(energy_count):
+        order += [(FEED_HOP, e, d) for d in range(1, groups)]
+        order += [(STEP, s, e) for s in range(sectors)]
+    return order
+
+
+def order_of(pairs, sectors, energy_count, groups):
+    plain = plain_order(pairs, sectors, energy_count, groups)
+    chosen = TUNED if sorted(TUNED) == sorted(plain) else plain
+    order, left = [], list(range(sectors))
+    for entry in chosen:
+        while left and entry[0] == STEP:
+            order.append((ANGLES, left.pop(0), 0))
+        order.append(entry)
+        if left:
+            order.append((ANGLES, left.pop(0), 0))
+    return order
 
 
 def sweep_kernel(
     sectors, groups, start, energies, limits, own_block, out,
     basis, amps, rotated, kept, turn, bounds,
-    local_sem, block_recv, side_send, over_send, up_send, down_send, core_send,
+    local_sem, block_recv, column_send, row_send, up_send, down_send, core_send,
     start_recv, start_up, start_down, bound_send, bound_recv, out_send, out_recv, out_local,
 ):
     k = lax.axis_index("sec")
@@ -98,8 +140,8 @@
     devices = sectors * groups
     has_up = z + 1 < groups
     has_down = z >= 1
-    rounds = max(pairs, energy_count)
-    inputs = 2 * rounds
+    piece = row_count // 4
+    order = order_of(pairs, sectors, energy_count, groups)
 
     def remote(src, dst, send, recv, **where):
         return pltpu.make_async_remote_copy(
@@ -114,44 +156,98 @@
         place = (k * groups + z + step) % devices
         return {"sec": place // groups, "ch": place % groups}
 
-    def block_move(s, b, send, **where):
-        part = basis.at[s, rows_of(b), :]
-        return remote(part, part, send.at[s // 2, b], block_recv.at[s, b], **where)
-
-    def routes(pair, b):
-        s = 2 * pair + core
-        across = pair % 2
-        near = jnp.where(across == 0, row == pair // 2, column == pair % 2)
-        carrier = near != (core == 1)
-        home = b == z
-        along = (s < last) & carrier
-        return s, [
-            (along & has_up & (b <= z), lambda: block_move(s, b, up_send, ch=z + 1)),
-            (along & has_down & (b >= z), lambda: block_move(s, b, down_send, ch=z - 1)),
-            (home & (chip == pair), lambda: block_move(s, b, side_send, sec=jnp.where(across == 0, column_peer, row_peer))),
-            (jnp.where(home, near, carrier), lambda: block_move(s, b, over_send, sec=jnp.where(across == 0, row_peer, column_peer))),
-            (b >= 0, lambda: block_move(s, b, core_send, sec=partner)),
-        ]
-
-    def travels(s, b):
-        return (s < last) | (b == z)
-
-    def relay(pair, b):
-        for wanted, move in routes(pair, b)[1]:
-            @pl.when(wanted)
-            def _():
-                move().start()
-
-    def block_arrived(s, b):
-        block_move(s, b, core_send, sec=partner).wait_recv()
-
-    def arrive_and_relay(pair, b):
-        s = 2 * pair + core
-
-        @pl.when((b >= 0) & (b < groups) & travels(s, b))
-        def _():
-            block_arrived(s, b)
-            relay(pair, b)
+    def part_of(s, b, q, h, count=1):
+        return basis.at[s, pl.ds(pl.multiple_of(b * row_count + (2 * q + h) * piece, piece), count * piece), :]
+
+    def piece_move(s, b, q, h, send, **where):
+        part = part_of(s, b, q, h)
+        return remote(part, part, send.at[s // 2, b], block_recv.at[s, b, 2 * q + h], **where)
+
+    def near(j, q):
+        return row == j // 2 if q == 0 else column == j % 2
+
+    def carried(j, q):
+        return jnp.where(near(j, q), 0, 1)
+
+    def lift(s, b, q, h):
+        @pl.when((s < last) & has_up & (b <= z))
+        def _():
+            piece_move(s, b, q, h, up_send, ch=z + 1).start()
+
+        @pl.when((s < last) & has_down & (b >= z))
+        def _():
+            piece_move(s, b, q, h, down_send, ch=z - 1).start()
+
+    def over(s, b, q, h):
+        if q == 0:
+            piece_move(s, b, q, h, row_send, sec=row_peer).start()
+        else:
+            piece_move(s, b, q, h, column_send, sec=column_peer).start()
+
+    def to_core(s, b, q, h):
+        piece_move(s, b, q, h, core_send, sec=partner).start()
+
+    def piece_arrived(s, b, q, h):
+        piece_move(s, b, q, h, core_send, sec=partner).wait_recv()
+
+    def give_own():
+        for h in (1, 0):
+            for q in range(2):
+                piece_move(k, z, q, h, column_send, sec=column_peer).start()
+                piece_move(k, z, q, h, row_send, sec=row_peer).start()
+        for h in (1, 0):
+            for q in range(2):
+                to_core(k, z, q, h)
+
+    def home(j):
+        s = 2 * j + core
+
+        @pl.when(chip != j)
+        def _():
+            for h in (1, 0):
+                for q in range(2):
+                    piece_arrived(s, z, q, h)
+
+                    @pl.when(near(j, q))
+                    def _():
+                        over(s, z, q, h)
+
+                    to_core(s, z, q, h)
+
+    def lift_own(j):
+        for q in range(2):
+            lift(2 * j + core, z, q, carried(j, q))
+
+    def hop_from(j, d):
+        s = 2 * j + core
+        for q in range(2):
+            for b in (z - d, z + d):
+                @pl.when((s < last) & (b >= 0) & (b < groups))
+                def _():
+                    h = carried(j, q)
+                    piece_arrived(s, b, q, h)
+                    lift(s, b, q, h)
+                    over(s, b, q, h)
+                    to_core(s, b, q, h)
+
+    def side_from(j, d):
+        s = 2 * j + core
+        for q in range(2):
+            for b in (z - d, z + d):
+                @pl.when((s < last) & (b >= 0) & (b < groups))
+                def _():
+                    h = 1 - carried(j, q)
+                    piece_arrived(s, b, q, h)
+                    to_core(s, b, q, h)
+
+    def twin(j):
+        s = 2 * j + 1 - core
+        for b in range(groups):
+            @pl.when((s < last) | (b == z))
+            def _():
+                for q in range(2):
+                    for h in range(2):
+                        piece_arrived(s, b, q, h)
 
     def start_part(e, c):
         return amps.at[0, e, rows_of(c), :]
@@ -173,39 +269,6 @@
         def _():
             start_move(e, c, start_up, sec=partner).wait_recv()
             start_relay(e, c)
-
-    def event(item, stage):
-        own = (stage == 0) & (item + 2 < inputs)
-        passed = (stage == 1) & (item + 1 < inputs)
-        hop = stage - 1
-        ahead = item + jnp.where(stage == 0, 2, jnp.where(stage == 1, 1, 0))
-        place = ahead // 2
-        is_pair = (ahead % 2 == 0) & (place < pairs)
-        is_start = (ahead % 2 == 1) & (place < energy_count)
-
-        @pl.when(is_pair & own & (chip == place))
-        def _():
-            relay(place, z)
-
-        @pl.when(is_pair & passed & (chip != place))
-        def _():
-            arrive_and_relay(place, z)
-
-        @pl.when(is_pair & (stage >= 2))
-        def _():
-            @pl.loop(0, 2)
-            def _(side):
-                arrive_and_relay(place, z - hop + 2 * hop * side)
-
-        @pl.when(is_start & own)
-        def _():
-            start_relay(place, z)
-
-        @pl.when(is_start & (stage >= 2))
-        def _():
-            @pl.loop(0, 2)
-            def _(side):
-                start_arrive_and_relay(place, z - hop + 2 * hop * side)
 
     loads = [
         pltpu.make_async_copy(own_block, basis.at[k, rows_of(z), :], local_sem.at[0]),
@@ -229,10 +292,7 @@
     pl.semaphore_wait(barrier, devices - 1)
     loads[0].wait()
 
-    @pl.when(chip == 0)
-    def _():
-        relay(0, z)
-
+    give_own()
     for load in loads[1:]:
         load.wait()
 
@@ -246,14 +306,7 @@
     def _(step):
         bound_move(step).start()
 
-    start_relay(0, z)
-
-    @pl.when(chip != 0)
-    def _():
-        arrive_and_relay(0, z)
-
-    @pl.loop(0, sectors)
-    def _(s):
+    def angles(s):
         for c in range(groups):
             @pl.when((s != k) | (c != z))
             def _():
@@ -310,59 +363,109 @@
             def _():
                 remote(kept.at[s, half, e], out.at[e, :, columns], out_send.at[s], out_recv.at[k], sec=s).start()
 
-    @pl.loop(0, inputs + 1)
-    def _(upcoming):
-        done = upcoming - 1
-        place = jnp.maximum(done, 0) // 2
-        from_pair = done % 2 == 0
-        ready = jnp.minimum(2 * place + 2, sectors)
-        pair_steps = jnp.where(place < pairs, 2 * jnp.minimum(place, energy_count), 0)
-        start_steps = jnp.where(place < energy_count, ready, 0)
-        steps = jnp.where(done < 0, 0, jnp.where(from_pair, pair_steps, start_steps))
-
-        def task(i):
-            return (
-                jnp.where(from_pair, 2 * place + i % 2, i),
-                jnp.where(from_pair, i // 2, place),
-            )
-
-        @pl.loop(0, jnp.maximum(steps + 1, STAGES))
-        def _(i):
-            @pl.when(i < steps)
-            def _():
-                advance(*task(i))
-
-            @pl.when((i >= 1) & (i <= steps))
-            def _():
-                send_out(*task(i - 1))
-
-            @pl.when((i < STAGES) & (upcoming < inputs))
-            def _():
-                event(upcoming, i)
-
-        @pl.when((upcoming % 2 == 0) & (upcoming // 2 < pairs))
-        def _():
-            s = 2 * (upcoming // 2) + 1 - core
-            for b in range(groups):
-                @pl.when(travels(s, b))
-                def _():
-                    block_arrived(s, b)
+    radix = max(sectors, energy_count, groups) + 1
+    codes = [(kind * radix + first) * radix + second for kind, first, second in (*order, (END, 0, 0))]
+    room = (END + 1) * radix * radix
+    packed = 2 if room**2 < 2**30 else 1
+    packed = 3 if room**3 < 2**30 else packed
+    words = [
+        sum(code * room**place for place, code in enumerate(codes[at : at + packed]))
+        for at in range(0, len(codes), packed)
+    ]
+
+    def entry(n):
+        word = jnp.int32(words[-1])
+        for at, value in enumerate(words[:-1]):
+            word = jnp.where(n // packed == at, value, word)
+        code = word % room
+        for place in range(1, packed):
+            code = jnp.where(n % packed == place, word // room**place % room, code)
+        return code // radix**2, code // radix % radix, code % radix
+
+    def act(n, before):
+        kind, first, second = entry(n)
+
+        @pl.when(kind == STEP)
+        def _():
+            advance(first, second)
+
+        @pl.when(kind == ANGLES)
+        def _():
+            angles(first)
+
+        @pl.when(kind == HOME)
+        def _():
+            home(first)
+
+        @pl.when(kind == LIFT)
+        def _():
+            lift_own(first)
+
+        @pl.when(kind == HOP)
+        def _():
+            hop_from(first, second)
+
+        @pl.when(kind == SIDE)
+        def _():
+            side_from(first, second)
+
+        @pl.when(kind == TWIN)
+        def _():
+            twin(first)
+
+        @pl.when(kind == FEED)
+        def _():
+            start_relay(first, z)
+
+        @pl.when(kind == FEED_HOP)
+        def _():
+            start_arrive_and_relay(first, z - second)
+            start_arrive_and_relay(first, z + second)
+
+        @pl.when(before[0] == STEP)
+        def _():
+            send_out(before[1], before[2])
+
+        return kind, first, second
+
+    lax.fori_loop(0, len(codes), act, (jnp.int32(END), jnp.int32(0), jnp.int32(0)))
 
     @pl.loop(1, devices)
     def _(step):
         bound_move(step).wait_send()
 
+    def drain(send, s, b, count, **where):
+        part = part_of(s, 0, 0, 0, count)
+        remote(part, part, send.at[s // 2, b], block_recv.at[s, b, 0], **where).wait_send()
+
     @pl.loop(0, pairs)
-    def _(pair):
+    def _(j):
+        s = 2 * j + core
         for b in range(groups):
-            s, moves = routes(pair, b)
-
-            @pl.when(travels(s, b))
-            def _():
-                for wanted, move in moves:
-                    @pl.when(wanted)
-                    def _():
-                        move().wait_send()
+            @pl.when((s < last) | (b == z))
+            def _():
+                drain(core_send, s, b, 4, sec=partner)
+
+            @pl.when((s < last) & has_up & (b <= z))
+            def _():
+                drain(up_send, s, b, 2, ch=z + 1)
+
+            @pl.when((s < last) & has_down & (b >= z))
+            def _():
+                drain(down_send, s, b, 2, ch=z - 1)
+
+            for send, target, turned in ((row_send, row_peer, 0), (column_send, column_peer, 1)):
+                @pl.when((b == z) & (chip == j))
+                def _():
+                    drain(send, s, b, 4, sec=target)
+
+                @pl.when((b == z) & (chip != j) & near(j, turned))
+                def _():
+                    drain(send, s, b, 2, sec=target)
+
+                @pl.when((b != z) & (s < last))
+                def _():
+                    drain(send, s, b, 1, sec=target)
 
     for c in range(groups):
         span = amps.at[0, :, pl.ds(c * row_count, row_count), :]
@@ -417,7 +520,7 @@
             pltpu.VMEM((sectors, energy_count, LANES, LANES), jnp.float32),
             pltpu.VMEM((sectors, groups, row_count // LANES, LANES), jnp.float32),
             dma((4,)),
-            dma((sectors, groups)),
+            dma((sectors, groups, 4)),
             dma((pairs, groups)),
             dma((pairs, groups)),
             dma((pairs, groups)),
@@ -447,7 +550,7 @@
     row_count, channel_count = intersection.shape[1:]
     gathered_bytes = sectors * channel_count**2 * intersection.dtype.itemsize
     even = sectors // 2 == 4 and (start_amps.shape[2] // 2) % (sectors * LANES) == 0
-    even = even and row_count % LANES == 0 and 3 * (channel_count // LANES) <= LANES
+    even = even and row_count % (4 * 16) == 0 and row_count % LANES == 0 and 3 * (channel_count // LANES) <= LANES
     if even and gathered_bytes <= GATHERED_LIMIT:
         return per_device_swept(start_amps, energies, thresholds, intersection)
     return per_device_pipelined(start_amps, energies, thresholds, intersection)

time: 310 us -> 202 us (0.65)
  Pallas kernels: 301 us -> 194 us
    pallas_call x1, Pallas kernels: 301 us -> 194 us  [per_device_swept(): pl.pallas_call(functools.partial(sweep_kernel, sectors, groups), out_shap...]
where the time goes in v2:
time: 202 us
  Pallas kernels  194 us (96%)
  local copies, waits for them, and re-layouts  6.61 us (3%)
    pallas_call x1, Pallas kernels, per_device_swept(): pl.pallas_call(functools.partial(sweep_kernel, sectors, groups), out_shap...  194 us
    unnamed x1, local copies, waits for them, and re-layouts  6.61 us

profile of v2, /device:TPU:7, one launch (start us, length us, event | category | flops | bytes accessed | tf_op | source)
XLA Modules:
  0.0 201.9 jit_solution(11178538503472004105)
XLA Ops:
  0.0 1.2 convert_element_type.7
  1.2 194.0 %shard_map.46 = bf16[6,256,2048]{2,1,0:T(8,128)(2,1)} custom-call(bf16[6,256,2048]{2,1,0:T(8,128)(2,1)} %start.1, f32[6]{0:T(128)} %energies.1, f32[2,128]{1,0:T(2,128)} %bitcast.5, bf16[256,1024]{1,0:T(8,128)(2,1)} %bitcast.4), custom_call_target="tpu_custom_call" | custom-call | tf_op jit(solution)/shard_map/pallas_call | solution.py:505
  195.3 6.6 %copy.6 = bf16[1,6,256,2048]{3,2,1,0:T(8,128)(2,1)} copy(bf16[1,6,256,2048]{3,2,1,0:T(8,128)(2,1)} %bitcast.3) | data formatting | bytes 12582912

commit v3 on v2

--- a/solution.py
+++ b/solution.py
@@ -1,4 +1,5 @@
 import functools
+import math
 import jax
 import jax.numpy as jnp
 from jax import lax
@@ -71,19 +72,18 @@
 
 
 LANES = 128
+PAIRED = 2
 HOME, LIFT, HOP, SIDE, TWIN, FEED, FEED_HOP, STEP, ANGLES, END = range(10)
 TUNED = (
-    (5, 0, 0), (5, 1, 0), (6, 0, 1), (6, 0, 2), (0, 0, 0), (1, 0, 0), (2, 0, 1), (3, 0, 1), (0, 1, 0), (2, 0, 2),
-    (1, 1, 0), (3, 0, 2), (2, 0, 3), (2, 1, 1), (0, 3, 0), (1, 3, 0), (2, 1, 2), (0, 2, 0), (2, 1, 3), (3, 1, 2),
-    (1, 2, 0), (3, 0, 3), (4, 0, 0), (3, 1, 1), (2, 2, 1), (2, 3, 1), (3, 1, 3), (2, 2, 2), (2, 3, 2), (3, 2, 1),
-    (3, 3, 1), (4, 1, 0), (6, 0, 3), (3, 2, 2), (2, 2, 3), (7, 0, 0), (2, 3, 3), (3, 2, 3), (3, 3, 2), (3, 3, 3),
-    (6, 1, 1), (5, 2, 0), (7, 1, 0), (7, 2, 0), (4, 2, 0), (6, 1, 2), (5, 3, 0), (7, 3, 0), (7, 4, 0), (6, 2, 1),
-    (7, 5, 0), (4, 3, 0), (7, 6, 0), (6, 1, 3), (7, 0, 1), (7, 7, 0), (7, 1, 1), (7, 2, 1), (6, 3, 1), (7, 3, 1),
-    (7, 4, 1), (6, 2, 2), (7, 5, 1), (6, 2, 3), (5, 4, 0), (6, 3, 2), (7, 6, 1), (7, 0, 2), (7, 7, 1), (5, 5, 0),
-    (7, 1, 2), (7, 2, 2), (6, 3, 3), (7, 3, 2), (7, 4, 2), (7, 0, 3), (6, 5, 1), (7, 1, 3), (6, 4, 1), (7, 5, 2),
-    (7, 6, 2), (6, 5, 2), (7, 2, 3), (7, 7, 2), (7, 3, 3), (7, 4, 3), (7, 5, 3), (7, 6, 3), (6, 4, 2), (6, 5, 3),
-    (7, 0, 5), (7, 1, 5), (6, 4, 3), (7, 7, 3), (7, 0, 4), (7, 2, 5), (7, 3, 5), (7, 1, 4), (7, 2, 4), (7, 4, 5),
-    (7, 5, 5), (7, 3, 4), (7, 4, 4), (7, 6, 5), (7, 5, 4), (7, 7, 5), (7, 6, 4), (7, 7, 4),
+    (5, 0, 0), (5, 3, 0), (6, 0, 1), (5, 1, 0), (6, 0, 2), (0, 1, 0), (1, 1, 0), (0, 2, 0), (1, 2, 0), (0, 0, 0),
+    (2, 1, 1), (2, 2, 1), (2, 2, 2), (1, 0, 0), (0, 3, 0), (2, 1, 2), (2, 0, 1), (2, 2, 3), (3, 1, 2), (2, 1, 3),
+    (2, 0, 2), (2, 0, 3), (3, 2, 1), (3, 1, 3), (1, 3, 0), (3, 2, 2), (3, 0, 2), (3, 0, 3), (3, 2, 3), (3, 1, 1),
+    (3, 0, 1), (2, 3, 1), (4, 1, 0), (2, 3, 2), (6, 1, 1), (2, 3, 3), (3, 3, 2), (6, 0, 3), (4, 2, 0), (4, 0, 0),
+    (6, 1, 2), (3, 3, 3), (3, 3, 1), (6, 1, 3), (7, 0, 0), (7, 1, 0), (7, 2, 0), (7, 3, 0), (7, 4, 0), (7, 5, 0),
+    (4, 3, 0), (5, 2, 0), (7, 6, 0), (6, 3, 1), (6, 3, 2), (7, 7, 0), (6, 2, 1), (5, 4, 0), (6, 3, 3), (6, 2, 2),
+    (5, 5, 0), (6, 2, 3), (7, 0, 1), (6, 4, 1), (7, 1, 1), (7, 2, 1), (7, 3, 1), (7, 4, 1), (6, 4, 2), (7, 5, 1),
+    (7, 6, 1), (6, 4, 3), (6, 5, 1), (7, 7, 1), (6, 5, 2), (6, 5, 3), (7, 0, 2), (7, 1, 2), (7, 2, 2), (7, 3, 2),
+    (7, 4, 2), (7, 5, 2), (7, 6, 2), (7, 7, 2),
 )
 
 
@@ -99,7 +99,8 @@
     order += [(TWIN, j, 0) for j in range(pairs)]
     for e in range(energy_count):
         order += [(FEED_HOP, e, d) for d in range(1, groups)]
-        order += [(STEP, s, e) for s in range(sectors)]
+        if (e + 1) % PAIRED == 0:
+            order += [(STEP, s, e // PAIRED) for s in range(sectors)]
     return order
 
 
@@ -114,6 +115,16 @@
         if left:
             order.append((ANGLES, left.pop(0), 0))
     return order
+
+
+def cos_and_sin(w):
+    u = (w - jnp.float32(1.57079637050628662109375)) + jnp.float32(4.37113900018624283e-8)
+    square = u * u
+    odd = even = None
+    for power in range(12, -1, -2):
+        even = (0.0 if even is None else even * square) + (-1.0) ** (power // 2) / math.factorial(power)
+        odd = (0.0 if odd is None else odd * square) + (-1.0) ** (power // 2) / math.factorial(power + 1)
+    return -u * odd, even
 
 
 def sweep_kernel(
@@ -270,6 +281,9 @@
             start_move(e, c, start_up, sec=partner).wait_recv()
             start_relay(e, c)
 
+    bounds[k, z] = jnp.concatenate(
+        [limits[:, q * LANES : (q + 1) * LANES] for q in range(row_count // LANES)], axis=0
+    ).astype(jnp.float32)
     loads = [
         pltpu.make_async_copy(own_block, basis.at[k, rows_of(z), :], local_sem.at[0]),
         pltpu.make_async_copy(
@@ -278,7 +292,6 @@
         pltpu.make_async_copy(
             start.at[:, :, pl.ds(pl.multiple_of(half_cols + k * width, width), width)],
             amps.at[0, :, rows_of(z), pl.ds(width, width)], local_sem.at[2]),
-        pltpu.make_async_copy(limits, bounds.at[k, z], local_sem.at[3]),
     ]
     for load in loads:
         load.start()
@@ -313,43 +326,50 @@
                 remote(bounds.at[s, c], bounds.at[s, c], bound_send.at[0], bound_recv.at[s, c], sec=partner).wait_recv()
 
         floor = jnp.concatenate([bounds[s, c] for c in range(groups)], axis=0)
+        wavenumber = jnp.concatenate([jnp.sqrt(energies[e] - floor) for e in range(energy_count)], axis=0)
+        cosine, sine = cos_and_sin(wavenumber)
+        shear, turned = (1.0 - cosine) / (wavenumber * sine), -wavenumber * sine
         for e in range(energy_count):
-            wavenumber = jnp.sqrt(energies[e] - floor)
-            cosine = jnp.cos(wavenumber)
-            sine_term = jnp.sin(wavenumber)
-            filler = jnp.zeros((LANES - 3 * chunks, LANES), jnp.float32)
-            stacked = jnp.concatenate(
-                [cosine, sine_term / wavenumber, -wavenumber * sine_term, filler], axis=0
-            )
-            turn[s, e] = stacked.T
-
-    def advance(s, e):
+            own = slice(e * chunks, (e + 1) * chunks)
+            turn[s, e] = jnp.concatenate([shear[own], turned[own]], axis=0).T
+
+    def rotate(s, e, m):
         source = jnp.minimum(s, 1)
         factors = turn[s, e]
         for q in range(chunks):
             place = pl.ds(q * LANES, LANES)
             both = amps[source, e, place, :].astype(jnp.float32)
+            shear, turned = factors[:, q : q + 1], factors[:, chunks + q : chunks + q + 1]
             values_part, slopes_part = both[:, :width], both[:, width:]
-            keep = factors[:, q : q + 1]
-            rise = factors[:, chunks + q : chunks + q + 1]
-            fall = factors[:, 2 * chunks + q : 2 * chunks + q + 1]
-            rotated[place, pl.ds(0, width)] = (keep * values_part + rise * slopes_part).astype(jnp.bfloat16)
-            rotated[place, pl.ds(width, width)] = (fall * values_part + keep * slopes_part).astype(jnp.bfloat16)
-
+            values_part = values_part + shear * slopes_part
+            slopes_part = slopes_part + turned * values_part
+            values_part = values_part + shear * slopes_part
+            rotated[m, place, pl.ds(0, width)] = values_part.astype(jnp.bfloat16)
+            rotated[m, place, pl.ds(width, width)] = slopes_part.astype(jnp.bfloat16)
+
+    def keep(s, e, mine):
+        kept[s, 0, e] = mine[:, :width]
+        kept[s, 1, e] = mine[:, width:]
+
+    def advance(s, group):
         @pl.when(s < last)
         def _():
-            amps[1, e] = jnp.dot(basis[s], rotated[...], preferred_element_type=jnp.float32).astype(jnp.bfloat16)
-            mine = amps[1, e, rows_of(z), :]
-            kept[s, 0, e] = mine[:, :width]
-            kept[s, 1, e] = mine[:, width:]
+            for m in range(PAIRED):
+                rotate(s, PAIRED * group + m, m)
+            for m in range(PAIRED):
+                e = PAIRED * group + m
+                amps[1, e] = jnp.dot(basis[s], rotated[m], preferred_element_type=jnp.float32).astype(jnp.bfloat16)
+            for m in range(PAIRED):
+                e = PAIRED * group + m
+                keep(s, e, amps[1, e, rows_of(z), :])
 
         @pl.when(s == last)
         def _():
-            mine = jnp.dot(
-                basis[s, rows_of(z), :], rotated[...], preferred_element_type=jnp.float32
-            ).astype(jnp.bfloat16)
-            kept[s, 0, e] = mine[:, :width]
-            kept[s, 1, e] = mine[:, width:]
+            for m in range(PAIRED):
+                rotate(s, PAIRED * group + m, m)
+            for m in range(PAIRED):
+                mine = jnp.dot(basis[s, rows_of(z), :], rotated[m], preferred_element_type=jnp.float32)
+                keep(s, PAIRED * group + m, mine.astype(jnp.bfloat16))
 
     def send_out(s, e):
         for half in range(2):
@@ -363,27 +383,39 @@
             def _():
                 remote(kept.at[s, half, e], out.at[e, :, columns], out_send.at[s], out_recv.at[k], sec=s).start()
 
-    radix = max(sectors, energy_count, groups) + 1
-    codes = [(kind * radix + first) * radix + second for kind, first, second in (*order, (END, 0, 0))]
-    room = (END + 1) * radix * radix
-    packed = 2 if room**2 < 2**30 else 1
-    packed = 3 if room**3 < 2**30 else packed
+    bits = max(sectors - 1, energy_count - 1, groups - 1).bit_length()
+    span = 2 * bits + END.bit_length()
+    packed = max(1, 30 // span)
+    codes = [(kind << 2 * bits) | (first << bits) | second for kind, first, second in (*order, (END, 0, 0))]
     words = [
-        sum(code * room**place for place, code in enumerate(codes[at : at + packed]))
+        sum(code << span * place for place, code in enumerate(codes[at : at + packed]))
         for at in range(0, len(codes), packed)
     ]
-
-    def entry(n):
-        word = jnp.int32(words[-1])
-        for at, value in enumerate(words[:-1]):
-            word = jnp.where(n // packed == at, value, word)
-        code = word % room
-        for place in range(1, packed):
-            code = jnp.where(n % packed == place, word // room**place % room, code)
-        return code // radix**2, code // radix % radix, code % radix
+    low = 2**bits
+
+    def entry(at, place):
+        values = words
+        while len(values) > 1:
+            odd = (at & 1) == 1
+            values = [
+                jnp.where(odd, values[i + 1], values[i]) if i + 1 < len(values) else values[i]
+                for i in range(0, len(values), 2)
+            ]
+            at = lax.shift_right_logical(at, jnp.int32(1))
+        word = values[0]
+        for step in range(1, packed):
+            word = jnp.where(place == step, lax.shift_right_logical(values[0], jnp.int32(span * step)), word)
+        word = word & (2**span - 1)
+        return (
+            lax.shift_right_logical(word, jnp.int32(2 * bits)),
+            lax.shift_right_logical(word, jnp.int32(bits)) & (low - 1),
+            word & (low - 1),
+        )
 
     def act(n, before):
-        kind, first, second = entry(n)
+        at, place = before[3:]
+        kind, first, second = entry(at, place)
+        wrapped = place == packed - 1
 
         @pl.when(kind == STEP)
         def _():
@@ -424,11 +456,12 @@
 
         @pl.when(before[0] == STEP)
         def _():
-            send_out(before[1], before[2])
-
-        return kind, first, second
-
-    lax.fori_loop(0, len(codes), act, (jnp.int32(END), jnp.int32(0), jnp.int32(0)))
+            for m in range(PAIRED):
+                send_out(before[1], PAIRED * before[2] + m)
+
+        return kind, first, second, jnp.where(wrapped, at + 1, at), jnp.where(wrapped, 0, place + 1)
+
+    lax.fori_loop(0, len(codes), act, (jnp.int32(END),) + (jnp.int32(0),) * 4)
 
     @pl.loop(1, devices)
     def _(step):
@@ -499,27 +532,26 @@
     channel_count = intersection.shape[2]
     width = width_cols // 2 // sectors
     pairs = sectors // 2
-    limits = thresholds.reshape(row_count // LANES, LANES).astype(jnp.float32)
     dma = pltpu.SemaphoreType.DMA
-    stored = jax.ShapeDtypeStruct(start_amps.shape, jnp.bfloat16)
+    stored = pltpu.VMEM(start_amps.shape, jnp.bfloat16)
     swept = pl.pallas_call(
         functools.partial(sweep_kernel, sectors, groups),
         out_shape=stored,
         in_specs=[
             pl.BlockSpec(memory_space=pl.ANY),
             pl.BlockSpec(memory_space=pltpu.SMEM),
-            pl.BlockSpec(memory_space=pl.ANY),
+            pl.BlockSpec(memory_space=pltpu.VMEM),
             pl.BlockSpec(memory_space=pl.ANY),
         ],
-        out_specs=pl.BlockSpec(memory_space=pl.ANY),
+        out_specs=pl.BlockSpec(memory_space=pltpu.VMEM),
         scratch_shapes=[
             pltpu.VMEM((sectors, channel_count, channel_count), jnp.bfloat16),
             pltpu.VMEM((2, energy_count, channel_count, 2 * width), jnp.bfloat16),
-            pltpu.VMEM((channel_count, 2 * width), jnp.bfloat16),
+            pltpu.VMEM((PAIRED, channel_count, 2 * width), jnp.bfloat16),
             pltpu.VMEM((sectors, 2, energy_count, row_count, width), jnp.bfloat16),
-            pltpu.VMEM((sectors, energy_count, LANES, LANES), jnp.float32),
+            pltpu.VMEM((sectors, energy_count, LANES, 2 * (channel_count // LANES)), jnp.float32),
             pltpu.VMEM((sectors, groups, row_count // LANES, LANES), jnp.float32),
-            dma((4,)),
+            dma((3,)),
             dma((sectors, groups, 4)),
             dma((pairs, groups)),
             dma((pairs, groups)),
@@ -536,9 +568,9 @@
             dma((1,)),
         ],
         compiler_params=pltpu.CompilerParams(
-            collective_id=0, has_side_effects=True, vmem_limit_bytes=60 * 2**20
+            collective_id=0, has_side_effects=True, vmem_limit_bytes=56 * 2**20
         ),
-    )(start_amps, energies, limits, intersection[0])
+    )(start_amps, energies, thresholds, intersection[0])
     return swept[None]
 
 
@@ -550,7 +582,7 @@
     row_count, channel_count = intersection.shape[1:]
     gathered_bytes = sectors * channel_count**2 * intersection.dtype.itemsize
     even = sectors // 2 == 4 and (start_amps.shape[2] // 2) % (sectors * LANES) == 0
-    even = even and row_count % (4 * 16) == 0 and row_count % LANES == 0 and 3 * (channel_count // LANES) <= LANES
+    even = even and energies.shape[0] % PAIRED == 0 and row_count % (4 * 16) == 0 and row_count % LANES == 0 and 3 * (channel_count // LANES) <= LANES
     if even and gathered_bytes <= GATHERED_LIMIT:
         return per_device_swept(start_amps, energies, thresholds, intersection)
     return per_device_pipelined(start_amps, energies, thresholds, intersection)

time: 202 us -> 190 us (0.941)
  Pallas kernels: 194 us -> 187 us
  local copies, waits for them, and re-layouts: 6.61 us -> 2.71 us
    pallas_call x1, Pallas kernels: 194 us -> 187 us  [per_device_swept(): pl.pallas_call(functools.partial(sweep_kernel, sectors, groups), out_shap...]
    unnamed x1, local copies, waits for them, and re-layouts: 6.61 us -> 2.71 us
where the time goes in v3:
time: 190 us; the launch traced here: 189 us
  Pallas kernels  187 us (98%)
  local copies, waits for them, and re-layouts  2.71 us (1%)
    pallas_call x1, Pallas kernels, per_device_swept(): pl.pallas_call(functools.partial(sweep_kernel, sectors, groups), out_shap...  187 us

profile of v3, /device:TPU:7, one launch (start us, length us, event | category | flops | bytes accessed | tf_op | source)
XLA Modules:
  0.0 189.4 jit_solution(670323942146947165)
XLA Ops:
  0.0 186.7 %shard_map.46 = bf16[6,256,2048]{2,1,0:T(8,128)(2,1)S(1)} custom-call(bf16[6,256,2048]{2,1,0:T(8,128)(2,1)} %start.1, f32[6]{0:T(128)} %energies.1, bf16[1,256]{1,0:T(2,128)(2,1)} %limits.1, bf16[256,1024]{1,0:T(8,128)(2,1)} %bitcast.3), custom_call_target="tpu_custom_call" | custom-call | tf_op jit(solution)/shard_map/pallas_call | solution.py:537
  186.7 2.7 %copy.6 = bf16[1,6,256,2048]{3,2,1,0:T(8,128)(2,1)} copy(bf16[1,6,256,2048]{3,2,1,0:T(8,128)(2,1)S(1)} %bitcast.2) | data formatting | bytes 12582912

commit v4 on v3

--- a/solution.py
+++ b/solution.py
@@ -73,29 +73,32 @@
 
 LANES = 128
 PAIRED = 2
-HOME, LIFT, HOP, SIDE, TWIN, FEED, FEED_HOP, STEP, ANGLES, END = range(10)
+QUARTERED = (0, 1)
+HOME, LIFT, HOP, SIDE, TWIN, FEED, FEED_HOP, STEP, FAR, ANGLES, END = range(11)
 TUNED = (
-    (5, 0, 0), (5, 3, 0), (6, 0, 1), (5, 1, 0), (6, 0, 2), (0, 1, 0), (1, 1, 0), (0, 2, 0), (1, 2, 0), (0, 0, 0),
-    (2, 1, 1), (2, 2, 1), (2, 2, 2), (1, 0, 0), (0, 3, 0), (2, 1, 2), (2, 0, 1), (2, 2, 3), (3, 1, 2), (2, 1, 3),
-    (2, 0, 2), (2, 0, 3), (3, 2, 1), (3, 1, 3), (1, 3, 0), (3, 2, 2), (3, 0, 2), (3, 0, 3), (3, 2, 3), (3, 1, 1),
-    (3, 0, 1), (2, 3, 1), (4, 1, 0), (2, 3, 2), (6, 1, 1), (2, 3, 3), (3, 3, 2), (6, 0, 3), (4, 2, 0), (4, 0, 0),
-    (6, 1, 2), (3, 3, 3), (3, 3, 1), (6, 1, 3), (7, 0, 0), (7, 1, 0), (7, 2, 0), (7, 3, 0), (7, 4, 0), (7, 5, 0),
-    (4, 3, 0), (5, 2, 0), (7, 6, 0), (6, 3, 1), (6, 3, 2), (7, 7, 0), (6, 2, 1), (5, 4, 0), (6, 3, 3), (6, 2, 2),
-    (5, 5, 0), (6, 2, 3), (7, 0, 1), (6, 4, 1), (7, 1, 1), (7, 2, 1), (7, 3, 1), (7, 4, 1), (6, 4, 2), (7, 5, 1),
-    (7, 6, 1), (6, 4, 3), (6, 5, 1), (7, 7, 1), (6, 5, 2), (6, 5, 3), (7, 0, 2), (7, 1, 2), (7, 2, 2), (7, 3, 2),
-    (7, 4, 2), (7, 5, 2), (7, 6, 2), (7, 7, 2),
+    (5, 0, 0), (6, 0, 1), (5, 1, 0), (6, 1, 1), (5, 2, 0), (0, 1, 0), (1, 1, 0), (0, 2, 0), (1, 2, 0), (0, 3, 0),
+    (0, 0, 0), (2, 1, 1), (1, 0, 0), (2, 1, 2), (2, 0, 1), (3, 1, 2), (2, 0, 2), (3, 0, 1), (2, 0, 3), (2, 1, 3),
+    (3, 1, 3), (1, 3, 0), (8, 1, 2), (6, 1, 2), (3, 0, 2), (3, 0, 3), (6, 1, 3), (2, 2, 1), (3, 1, 1), (2, 3, 1),
+    (2, 3, 2), (8, 0, 1), (2, 3, 3), (8, 0, 3), (2, 2, 2), (8, 0, 2), (2, 2, 3), (6, 0, 2), (8, 1, 3), (3, 3, 1),
+    (8, 1, 1), (6, 2, 1), (3, 2, 1), (6, 0, 3), (4, 0, 0), (7, 0, 0), (3, 3, 2), (3, 3, 3), (3, 2, 2), (5, 3, 0),
+    (3, 2, 3), (7, 1, 0), (4, 1, 0), (7, 2, 0), (6, 2, 2), (7, 3, 0), (4, 3, 0), (4, 2, 0), (7, 4, 0), (7, 5, 0),
+    (7, 6, 0), (6, 2, 3), (6, 3, 1), (7, 7, 0), (5, 4, 0), (6, 3, 2), (6, 4, 1), (6, 3, 3), (7, 0, 1), (7, 1, 1),
+    (7, 2, 1), (6, 4, 2), (5, 5, 0), (7, 3, 1), (7, 4, 1), (7, 5, 1), (7, 6, 1), (6, 5, 1), (6, 5, 2), (6, 5, 3),
+    (6, 4, 3), (7, 0, 2), (7, 1, 2), (7, 7, 1), (7, 2, 2), (7, 3, 2), (7, 4, 2), (7, 5, 2), (7, 6, 2), (7, 7, 2),
 )
 
 
 def plain_order(pairs, sectors, energy_count, groups):
     order = [(HOME, j, 0) for j in range(pairs)]
     order += [(FEED, e, 0) for e in range(energy_count)] + [(LIFT, j, 0) for j in range(pairs)]
-    for tick in range(pairs + groups):
+    for tick in range(pairs + groups + 1):
         for d in range(groups - 1, 0, -1):
             if 0 <= tick - d < pairs:
                 order.append((HOP, tick - d, d))
             if 0 <= tick - d - 1 < pairs:
                 order.append((SIDE, tick - d - 1, d))
+            if 0 <= tick - d - 2 < pairs and tick - d - 2 in QUARTERED:
+                order.append((FAR, tick - d - 2, d))
     order += [(TWIN, j, 0) for j in range(pairs)]
     for e in range(energy_count):
         order += [(FEED_HOP, e, d) for d in range(1, groups)]
@@ -167,98 +170,158 @@
         place = (k * groups + z + step) % devices
         return {"sec": place // groups, "ch": place % groups}
 
-    def part_of(s, b, q, h, count=1):
-        return basis.at[s, pl.ds(pl.multiple_of(b * row_count + (2 * q + h) * piece, piece), count * piece), :]
-
-    def piece_move(s, b, q, h, send, **where):
-        part = part_of(s, b, q, h)
-        return remote(part, part, send.at[s // 2, b], block_recv.at[s, b, 2 * q + h], **where)
+    def part_of(s, b, r, count=1):
+        return basis.at[s, pl.ds(pl.multiple_of(b * row_count + r * piece, piece), count * piece), :]
+
+    def piece_move(s, b, r, send, **where):
+        part = part_of(s, b, r)
+        return remote(part, part, send.at[s // 2, b], block_recv.at[s, b, r], **where)
+
+    column_chip, row_chip = chip + 1 - 2 * column, chip + 2 - 4 * row
+
+    def quartered(j):
+        found = j < 0
+        for pair in QUARTERED:
+            found = found | (j == pair)
+        return found
 
     def near(j, q):
         return row == j // 2 if q == 0 else column == j % 2
 
     def carried(j, q):
-        return jnp.where(near(j, q), 0, 1)
-
-    def lift(s, b, q, h):
+        return jnp.where(near(j, q), 2 * q, 2 * q + 1)
+
+    def left_over(j, q):
+        return jnp.where(near(j, q), 2 * q + 1, 2 * q)
+
+    def lift(s, b, r):
         @pl.when((s < last) & has_up & (b <= z))
         def _():
-            piece_move(s, b, q, h, up_send, ch=z + 1).start()
+            piece_move(s, b, r, up_send, ch=z + 1).start()
 
         @pl.when((s < last) & has_down & (b >= z))
         def _():
-            piece_move(s, b, q, h, down_send, ch=z - 1).start()
-
-    def over(s, b, q, h):
-        if q == 0:
-            piece_move(s, b, q, h, row_send, sec=row_peer).start()
-        else:
-            piece_move(s, b, q, h, column_send, sec=column_peer).start()
-
-    def to_core(s, b, q, h):
-        piece_move(s, b, q, h, core_send, sec=partner).start()
-
-    def piece_arrived(s, b, q, h):
-        piece_move(s, b, q, h, core_send, sec=partner).wait_recv()
+            piece_move(s, b, r, down_send, ch=z - 1).start()
+
+    def to_column(s, b, r):
+        piece_move(s, b, r, column_send, sec=column_peer).start()
+
+    def to_row(s, b, r):
+        piece_move(s, b, r, row_send, sec=row_peer).start()
+
+    def to_core(s, b, r):
+        piece_move(s, b, r, core_send, sec=partner).start()
+
+    def piece_arrived(s, b, r):
+        piece_move(s, b, r, core_send, sec=partner).wait_recv()
 
     def give_own():
-        for h in (1, 0):
-            for q in range(2):
-                piece_move(k, z, q, h, column_send, sec=column_peer).start()
-                piece_move(k, z, q, h, row_send, sec=row_peer).start()
-        for h in (1, 0):
-            for q in range(2):
-                to_core(k, z, q, h)
+        for r in (1, 3, 0, 2):
+            to_column(k, z, r)
+            to_row(k, z, r)
+        for r in (1, 3, 0, 2):
+            to_core(k, z, r)
 
     def home(j):
         s = 2 * j + core
 
         @pl.when(chip != j)
         def _():
-            for h in (1, 0):
-                for q in range(2):
-                    piece_arrived(s, z, q, h)
-
-                    @pl.when(near(j, q))
-                    def _():
-                        over(s, z, q, h)
-
-                    to_core(s, z, q, h)
+            for r in (1, 3, 0, 2):
+                piece_arrived(s, z, r)
+
+                @pl.when(near(j, r // 2))
+                def _():
+                    (to_column if r // 2 else to_row)(s, z, r)
+
+                to_core(s, z, r)
 
     def lift_own(j):
-        for q in range(2):
-            lift(2 * j + core, z, q, carried(j, q))
+        @pl.when(quartered(j))
+        def _():
+            lift(2 * j + core, z, chip)
+
+        @pl.when(~quartered(j))
+        def _():
+            for q in range(2):
+                lift(2 * j + core, z, carried(j, q))
+
+    def both_sides(j, d, action):
+        s = 2 * j + core
+        for b in (z - d, z + d):
+            @pl.when((s < last) & (b >= 0) & (b < groups))
+            def _():
+                action(s, b)
 
     def hop_from(j, d):
-        s = 2 * j + core
-        for q in range(2):
-            for b in (z - d, z + d):
-                @pl.when((s < last) & (b >= 0) & (b < groups))
+        @pl.when(quartered(j))
+        def _():
+            def action(s, b):
+                piece_arrived(s, b, chip)
+                lift(s, b, chip)
+                to_column(s, b, chip)
+                to_row(s, b, chip)
+                to_core(s, b, chip)
+
+            both_sides(j, d, action)
+
+        @pl.when(~quartered(j))
+        def _():
+            for q in range(2):
+                def action(s, b):
+                    r = carried(j, q)
+                    piece_arrived(s, b, r)
+                    lift(s, b, r)
+                    (to_column if q else to_row)(s, b, r)
+                    to_core(s, b, r)
+
+                both_sides(j, d, action)
+
+    def side_from(j, d):
+        @pl.when(quartered(j))
+        def _():
+            def action(s, b):
+                piece_arrived(s, b, column_chip)
+
+                @pl.when(core == 1)
                 def _():
-                    h = carried(j, q)
-                    piece_arrived(s, b, q, h)
-                    lift(s, b, q, h)
-                    over(s, b, q, h)
-                    to_core(s, b, q, h)
-
-    def side_from(j, d):
-        s = 2 * j + core
-        for q in range(2):
-            for b in (z - d, z + d):
-                @pl.when((s < last) & (b >= 0) & (b < groups))
+                    to_row(s, b, column_chip)
+
+                to_core(s, b, column_chip)
+                piece_arrived(s, b, row_chip)
+
+                @pl.when(core == 0)
                 def _():
-                    h = 1 - carried(j, q)
-                    piece_arrived(s, b, q, h)
-                    to_core(s, b, q, h)
+                    to_column(s, b, row_chip)
+
+                to_core(s, b, row_chip)
+
+            both_sides(j, d, action)
+
+        @pl.when(~quartered(j))
+        def _():
+            for q in range(2):
+                def action(s, b):
+                    r = left_over(j, q)
+                    piece_arrived(s, b, r)
+                    to_core(s, b, r)
+
+                both_sides(j, d, action)
+
+    def far_from(j, d):
+        def action(s, b):
+            piece_arrived(s, b, 3 - chip)
+            to_core(s, b, 3 - chip)
+
+        both_sides(j, d, action)
 
     def twin(j):
         s = 2 * j + 1 - core
         for b in range(groups):
             @pl.when((s < last) | (b == z))
             def _():
-                for q in range(2):
-                    for h in range(2):
-                        piece_arrived(s, b, q, h)
+                for r in range(4):
+                    piece_arrived(s, b, r)
 
     def start_part(e, c):
         return amps.at[0, e, rows_of(c), :]
@@ -441,6 +504,10 @@
         def _():
             side_from(first, second)
 
+        @pl.when(kind == FAR)
+        def _():
+            far_from(first, second)
+
         @pl.when(kind == TWIN)
         def _():
             twin(first)
@@ -468,7 +535,7 @@
         bound_move(step).wait_send()
 
     def drain(send, s, b, count, **where):
-        part = part_of(s, 0, 0, 0, count)
+        part = part_of(s, 0, 0, count)
         remote(part, part, send.at[s // 2, b], block_recv.at[s, b, 0], **where).wait_send()
 
     @pl.loop(0, pairs)
@@ -479,13 +546,14 @@
             def _():
                 drain(core_send, s, b, 4, sec=partner)
 
-            @pl.when((s < last) & has_up & (b <= z))
-            def _():
-                drain(up_send, s, b, 2, ch=z + 1)
-
-            @pl.when((s < last) & has_down & (b >= z))
-            def _():
-                drain(down_send, s, b, 2, ch=z - 1)
+            for pieces, wanted in ((1, quartered(j)), (2, ~quartered(j))):
+                @pl.when((s < last) & has_up & (b <= z) & wanted)
+                def _():
+                    drain(up_send, s, b, pieces, ch=z + 1)
+
+                @pl.when((s < last) & has_down & (b >= z) & wanted)
+                def _():
+                    drain(down_send, s, b, pieces, ch=z - 1)
 
             for send, target, turned in ((row_send, row_peer, 0), (column_send, column_peer, 1)):
                 @pl.when((b == z) & (chip == j))
@@ -496,9 +564,12 @@
                 def _():
                     drain(send, s, b, 2, sec=target)
 
-                @pl.when((b != z) & (s < last))
-                def _():
-                    drain(send, s, b, 1, sec=target)
+                twice = quartered(j) & (core == 1 - turned)
+
+                for pieces, wanted in ((2, twice), (1, ~twice)):
+                    @pl.when((b != z) & (s < last) & wanted)
+                    def _():
+                        drain(send, s, b, pieces, sec=target)
 
     for c in range(groups):
         span = amps.at[0, :, pl.ds(c * row_count, row_count), :]

time: 190 us -> 174 us (0.916)
  Pallas kernels: 187 us -> 171 us
    pallas_call x1, Pallas kernels: 187 us -> 171 us  [per_device_swept(): pl.pallas_call(functools.partial(sweep_kernel, sectors, groups), out_shap...]
where the time goes in v4:
time: 174 us
  Pallas kernels  171 us (98%)
  local copies, waits for them, and re-layouts  2.71 us (2%)
    pallas_call x1, Pallas kernels, per_device_swept(): pl.pallas_call(functools.partial(sweep_kernel, sectors, groups), out_shap...  171 us

profile of v4, /device:TPU:7, one launch (start us, length us, event | category | flops | bytes accessed | tf_op | source)
XLA Modules:
  0.0 174.2 jit_solution(14150693196008168615)
XLA Ops:
  0.0 171.5 %shard_map.46 = bf16[6,256,2048]{2,1,0:T(8,128)(2,1)S(1)} custom-call(bf16[6,256,2048]{2,1,0:T(8,128)(2,1)} %start.1, f32[6]{0:T(128)} %energies.1, bf16[1,256]{1,0:T(2,128)(2,1)} %limits.1, bf16[256,1024]{1,0:T(8,128)(2,1)} %bitcast.3), custom_call_target="tpu_custom_call" | custom-call | tf_op jit(solution)/shard_map/pallas_call | solution.py:608
  171.5 2.7 %copy.6 = bf16[1,6,256,2048]{3,2,1,0:T(8,128)(2,1)} copy(bf16[1,6,256,2048]{3,2,1,0:T(8,128)(2,1)S(1)} %bitcast.2) | data formatting | bytes 12582912

commit v5 on v4

--- a/solution.py
+++ b/solution.py
@@ -73,24 +73,27 @@
 
 LANES = 128
 PAIRED = 2
+EXTRA = 2
 QUARTERED = (0, 1)
 HOME, LIFT, HOP, SIDE, TWIN, FEED, FEED_HOP, STEP, FAR, ANGLES, END = range(11)
 TUNED = (
-    (5, 0, 0), (6, 0, 1), (5, 1, 0), (6, 1, 1), (5, 2, 0), (0, 1, 0), (1, 1, 0), (0, 2, 0), (1, 2, 0), (0, 3, 0),
-    (0, 0, 0), (2, 1, 1), (1, 0, 0), (2, 1, 2), (2, 0, 1), (3, 1, 2), (2, 0, 2), (3, 0, 1), (2, 0, 3), (2, 1, 3),
-    (3, 1, 3), (1, 3, 0), (8, 1, 2), (6, 1, 2), (3, 0, 2), (3, 0, 3), (6, 1, 3), (2, 2, 1), (3, 1, 1), (2, 3, 1),
-    (2, 3, 2), (8, 0, 1), (2, 3, 3), (8, 0, 3), (2, 2, 2), (8, 0, 2), (2, 2, 3), (6, 0, 2), (8, 1, 3), (3, 3, 1),
-    (8, 1, 1), (6, 2, 1), (3, 2, 1), (6, 0, 3), (4, 0, 0), (7, 0, 0), (3, 3, 2), (3, 3, 3), (3, 2, 2), (5, 3, 0),
-    (3, 2, 3), (7, 1, 0), (4, 1, 0), (7, 2, 0), (6, 2, 2), (7, 3, 0), (4, 3, 0), (4, 2, 0), (7, 4, 0), (7, 5, 0),
-    (7, 6, 0), (6, 2, 3), (6, 3, 1), (7, 7, 0), (5, 4, 0), (6, 3, 2), (6, 4, 1), (6, 3, 3), (7, 0, 1), (7, 1, 1),
-    (7, 2, 1), (6, 4, 2), (5, 5, 0), (7, 3, 1), (7, 4, 1), (7, 5, 1), (7, 6, 1), (6, 5, 1), (6, 5, 2), (6, 5, 3),
-    (6, 4, 3), (7, 0, 2), (7, 1, 2), (7, 7, 1), (7, 2, 2), (7, 3, 2), (7, 4, 2), (7, 5, 2), (7, 6, 2), (7, 7, 2),
+    (5, 0, 0), (5, 1, 0), (6, 1, 1), (6, 0, 1), (6, 1, 2), (5, 2, 0), (0, 2, 0), (1, 2, 0), (0, 1, 0), (1, 1, 0),
+    (0, 0, 0), (0, 3, 0), (2, 1, 1), (2, 1, 2), (1, 0, 0), (2, 1, 3), (3, 1, 1), (2, 0, 1), (2, 0, 2), (8, 1, 1),
+    (3, 1, 3), (2, 0, 3), (3, 1, 2), (1, 3, 0), (2, 2, 1), (3, 0, 3), (2, 3, 1), (2, 3, 2), (3, 0, 2), (3, 2, 1),
+    (3, 0, 1), (8, 0, 3), (8, 1, 2), (6, 0, 2), (6, 0, 3), (8, 1, 3), (2, 3, 3), (6, 1, 3), (2, 2, 2), (3, 3, 2),
+    (8, 0, 2), (8, 0, 1), (5, 7, 0), (2, 2, 3), (6, 2, 1), (5, 4, 0), (3, 3, 1), (4, 1, 0), (4, 0, 0), (7, 0, 0),
+    (3, 2, 2), (5, 3, 0), (3, 2, 3), (7, 1, 0), (7, 2, 0), (3, 3, 3), (7, 3, 0), (6, 2, 2), (4, 3, 0), (4, 2, 0),
+    (7, 4, 0), (6, 4, 1), (7, 5, 0), (7, 6, 0), (6, 3, 1), (7, 7, 0), (6, 2, 3), (6, 3, 2), (5, 5, 0), (6, 3, 3),
+    (7, 0, 1), (7, 1, 1), (7, 2, 1), (7, 3, 1), (6, 4, 2), (6, 5, 1), (7, 4, 1), (5, 6, 0), (7, 5, 1), (6, 5, 2),
+    (7, 6, 1), (6, 7, 1), (6, 5, 3), (7, 7, 1), (6, 4, 3), (6, 6, 1), (6, 7, 2), (7, 0, 2), (7, 1, 2), (6, 6, 2),
+    (7, 2, 2), (7, 3, 2), (7, 4, 2), (6, 7, 3), (6, 6, 3), (7, 5, 2), (7, 0, 3), (7, 6, 2), (7, 1, 3), (7, 2, 3),
+    (7, 7, 2), (7, 3, 3), (7, 4, 3), (7, 5, 3), (7, 6, 3), (7, 7, 3),
 )
 
 
 def plain_order(pairs, sectors, energy_count, groups):
     order = [(HOME, j, 0) for j in range(pairs)]
-    order += [(FEED, e, 0) for e in range(energy_count)] + [(LIFT, j, 0) for j in range(pairs)]
+    order += [(FEED, e, 0) for e in range(energy_count + EXTRA)] + [(LIFT, j, 0) for j in range(pairs)]
     for tick in range(pairs + groups + 1):
         for d in range(groups - 1, 0, -1):
             if 0 <= tick - d < pairs:
@@ -100,7 +103,7 @@
             if 0 <= tick - d - 2 < pairs and tick - d - 2 in QUARTERED:
                 order.append((FAR, tick - d - 2, d))
     order += [(TWIN, j, 0) for j in range(pairs)]
-    for e in range(energy_count):
+    for e in range(energy_count + EXTRA):
         order += [(FEED_HOP, e, d) for d in range(1, groups)]
         if (e + 1) % PAIRED == 0:
             order += [(STEP, s, e // PAIRED) for s in range(sectors)]
@@ -132,9 +135,9 @@
 
 def sweep_kernel(
     sectors, groups, start, energies, limits, own_block, out,
-    basis, amps, rotated, kept, turn, bounds,
+    basis, amps, rotated, kept, doubled, turn, bounds,
     local_sem, block_recv, column_send, row_send, up_send, down_send, core_send,
-    start_recv, start_up, start_down, bound_send, bound_recv, out_send, out_recv, out_local,
+    start_recv, start_up, start_down, bound_send, bound_recv, out_send, out_recv, out_local, doubled_sem,
 ):
     k = lax.axis_index("sec")
     z = lax.axis_index("ch")
@@ -152,6 +155,9 @@
     channel_count = row_count * groups
     chunks = channel_count // LANES
     devices = sectors * groups
+    across = column_peer + row_peer - k
+    across_chip = across // 2
+    shared = energy_count - EXTRA
     has_up = z + 1 < groups
     has_down = z >= 1
     piece = row_count // 4
@@ -349,13 +355,15 @@
     ).astype(jnp.float32)
     loads = [
         pltpu.make_async_copy(own_block, basis.at[k, rows_of(z), :], local_sem.at[0]),
-        pltpu.make_async_copy(
-            start.at[:, :, pl.ds(pl.multiple_of(k * width, width), width)],
-            amps.at[0, :, rows_of(z), pl.ds(0, width)], local_sem.at[1]),
-        pltpu.make_async_copy(
-            start.at[:, :, pl.ds(pl.multiple_of(half_cols + k * width, width), width)],
-            amps.at[0, :, rows_of(z), pl.ds(width, width)], local_sem.at[2]),
     ]
+    for half in range(2):
+        for owner, source, target in (
+            (k, pl.ds(0, energy_count), pl.ds(0, energy_count)),
+            (across, pl.ds(shared, EXTRA), pl.ds(energy_count, EXTRA)),
+        ):
+            loads.append(pltpu.make_async_copy(
+                start.at[source, :, pl.ds(pl.multiple_of(half * half_cols + owner * width, width), width)],
+                amps.at[0, target, rows_of(z), pl.ds(half * width, width)], local_sem.at[len(loads)]))
     for load in loads:
         load.start()
 
@@ -398,7 +406,7 @@
 
     def rotate(s, e, m):
         source = jnp.minimum(s, 1)
-        factors = turn[s, e]
+        factors = turn[s, jnp.where(e < energy_count, e, e - EXTRA)]
         for q in range(chunks):
             place = pl.ds(q * LANES, LANES)
             both = amps[source, e, place, :].astype(jnp.float32)
@@ -410,43 +418,72 @@
             rotated[m, place, pl.ds(0, width)] = values_part.astype(jnp.bfloat16)
             rotated[m, place, pl.ds(width, width)] = slopes_part.astype(jnp.bfloat16)
 
-    def keep(s, e, mine):
-        kept[s, 0, e] = mine[:, :width]
-        kept[s, 1, e] = mine[:, width:]
+    def keep(s, group, mine_of):
+        @pl.when(group < energy_count // PAIRED)
+        def _():
+            for m in range(PAIRED):
+                mine = mine_of(m)
+                kept[s, 0, PAIRED * group + m] = mine[:, :width]
+                kept[s, 1, PAIRED * group + m] = mine[:, width:]
+
+        @pl.when((group >= energy_count // PAIRED) & (s // 2 == chip))
+        def _():
+            for m in range(PAIRED):
+                mine = mine_of(m)
+                doubled[s % 2, 0, PAIRED * group + m - energy_count] = mine[:, :width]
+                doubled[s % 2, 1, PAIRED * group + m - energy_count] = mine[:, width:]
 
     def advance(s, group):
-        @pl.when(s < last)
+        wanted = (group < energy_count // PAIRED) | (s // 2 <= chip)
+
+        @pl.when(wanted & (s < last))
         def _():
             for m in range(PAIRED):
                 rotate(s, PAIRED * group + m, m)
             for m in range(PAIRED):
                 e = PAIRED * group + m
                 amps[1, e] = jnp.dot(basis[s], rotated[m], preferred_element_type=jnp.float32).astype(jnp.bfloat16)
-            for m in range(PAIRED):
-                e = PAIRED * group + m
-                keep(s, e, amps[1, e, rows_of(z), :])
-
-        @pl.when(s == last)
+            keep(s, group, lambda m: amps[1, PAIRED * group + m, rows_of(z), :])
+
+        @pl.when(wanted & (s == last))
         def _():
             for m in range(PAIRED):
                 rotate(s, PAIRED * group + m, m)
             for m in range(PAIRED):
                 mine = jnp.dot(basis[s, rows_of(z), :], rotated[m], preferred_element_type=jnp.float32)
-                keep(s, PAIRED * group + m, mine.astype(jnp.bfloat16))
+                amps[1, PAIRED * group + m, rows_of(z), :] = mine.astype(jnp.bfloat16)
+            keep(s, group, lambda m: amps[1, PAIRED * group + m, rows_of(z), :])
+
+    def columns_of(owner, half):
+        return pl.ds(pl.multiple_of(half * half_cols + owner * width, width), width)
 
     def send_out(s, e):
         for half in range(2):
-            columns = pl.ds(pl.multiple_of(half * half_cols + k * width, width), width)
+            part = kept.at[s, half, e]
+            place = out.at[e, :, columns_of(k, half)]
 
             @pl.when(s == k)
             def _():
-                pltpu.make_async_copy(kept.at[s, half, e], out.at[e, :, columns], out_local.at[0]).start()
-
-            @pl.when(s != k)
-            def _():
-                remote(kept.at[s, half, e], out.at[e, :, columns], out_send.at[s], out_recv.at[k], sec=s).start()
-
-    bits = max(sectors - 1, energy_count - 1, groups - 1).bit_length()
+                pltpu.make_async_copy(part, place, out_local.at[0]).start()
+
+            @pl.when((s != k) & ((e < shared) | (s // 2 != across_chip)))
+            def _():
+                remote(part, place, out_send.at[s], out_recv.at[k], sec=s).start()
+
+    def send_doubled(s, e):
+        for half in range(2):
+            part = doubled.at[s % 2, half, e - energy_count]
+            place = out.at[e - EXTRA, :, columns_of(across, half)]
+
+            @pl.when(s == k)
+            def _():
+                pltpu.make_async_copy(part, place, doubled_sem.at[0]).start()
+
+            @pl.when(s == partner)
+            def _():
+                remote(part, place, doubled_sem.at[1], doubled_sem.at[2], sec=partner).start()
+
+    bits = max(sectors - 1, energy_count + EXTRA - 1, groups - 1).bit_length()
     span = 2 * bits + END.bit_length()
     packed = max(1, 30 // span)
     codes = [(kind << 2 * bits) | (first << bits) | second for kind, first, second in (*order, (END, 0, 0))]
@@ -523,8 +560,15 @@
 
         @pl.when(before[0] == STEP)
         def _():
-            for m in range(PAIRED):
-                send_out(before[1], PAIRED * before[2] + m)
+            @pl.when(before[2] < energy_count // PAIRED)
+            def _():
+                for m in range(PAIRED):
+                    send_out(before[1], PAIRED * before[2] + m)
+
+            @pl.when(before[2] >= energy_count // PAIRED)
+            def _():
+                for m in range(PAIRED):
+                    send_doubled(before[1], PAIRED * before[2] + m)
 
         return kind, first, second, jnp.where(wrapped, at + 1, at), jnp.where(wrapped, 0, place + 1)
 
@@ -584,16 +628,23 @@
 
     @pl.loop(0, sectors)
     def _(s):
-        whole = remote(kept.at[s], kept.at[s], out_send.at[s], out_recv.at[s], sec=partner)
-
-        @pl.when(s != k)
-        def _():
-            whole.wait_send()
-            whole.wait_recv()
-
         @pl.when(s == k)
         def _():
             pltpu.make_async_copy(kept.at[s], kept.at[s], out_local.at[0]).wait()
+
+        for far in range(2):
+            part = kept.at[s, :, pl.ds(0, shared if far else energy_count)]
+            move = remote(part, part, out_send.at[s], out_recv.at[s], sec=partner)
+
+            @pl.when((s != k) & (s // 2 == across_chip if far else s // 2 != across_chip))
+            def _():
+                move.wait_send()
+                move.wait_recv()
+
+    pltpu.make_async_copy(doubled.at[0], doubled.at[0], doubled_sem.at[0]).wait()
+    crossed = remote(doubled.at[0], doubled.at[0], doubled_sem.at[1], doubled_sem.at[2], sec=partner)
+    crossed.wait_send()
+    crossed.wait_recv()
 
 
 def per_device_swept(start_amps, energies, thresholds, intersection):
@@ -617,19 +668,20 @@
         out_specs=pl.BlockSpec(memory_space=pltpu.VMEM),
         scratch_shapes=[
             pltpu.VMEM((sectors, channel_count, channel_count), jnp.bfloat16),
-            pltpu.VMEM((2, energy_count, channel_count, 2 * width), jnp.bfloat16),
+            pltpu.VMEM((2, energy_count + EXTRA, channel_count, 2 * width), jnp.bfloat16),
             pltpu.VMEM((PAIRED, channel_count, 2 * width), jnp.bfloat16),
             pltpu.VMEM((sectors, 2, energy_count, row_count, width), jnp.bfloat16),
+            pltpu.VMEM((2, 2, EXTRA, row_count, width), jnp.bfloat16),
             pltpu.VMEM((sectors, energy_count, LANES, 2 * (channel_count // LANES)), jnp.float32),
             pltpu.VMEM((sectors, groups, row_count // LANES, LANES), jnp.float32),
-            dma((3,)),
+            dma((5,)),
             dma((sectors, groups, 4)),
             dma((pairs, groups)),
             dma((pairs, groups)),
             dma((pairs, groups)),
             dma((pairs, groups)),
             dma((pairs, groups)),
-            dma((energy_count, groups)),
+            dma((energy_count + EXTRA, groups)),
             dma((groups,)),
             dma((groups,)),
             dma((sectors * groups,)),
@@ -637,6 +689,7 @@
             dma((sectors,)),
             dma((sectors,)),
             dma((1,)),
+            dma((3,)),
         ],
         compiler_params=pltpu.CompilerParams(
             collective_id=0, has_side_effects=True, vmem_limit_bytes=56 * 2**20
@@ -653,7 +706,7 @@
     row_count, channel_count = intersection.shape[1:]
     gathered_bytes = sectors * channel_count**2 * intersection.dtype.itemsize
     even = sectors // 2 == 4 and (start_amps.shape[2] // 2) % (sectors * LANES) == 0
-    even = even and energies.shape[0] % PAIRED == 0 and row_count % (4 * 16) == 0 and row_count % LANES == 0 and 3 * (channel_count // LANES) <= LANES
+    even = even and energies.shape[0] % PAIRED == 0 and energies.shape[0] > EXTRA and row_count % (4 * 16) == 0 and row_count % LANES == 0 and 3 * (channel_count // LANES) <= LANES
     if even and gathered_bytes <= GATHERED_LIMIT:
         return per_device_swept(start_amps, energies, thresholds, intersection)
     return per_device_pipelined(start_amps, energies, thresholds, intersection)

time: 174 us -> 166 us (0.954)
  Pallas kernels: 171 us -> 163 us
    pallas_call x1, Pallas kernels: 171 us -> 163 us  [per_device_swept(): pl.pallas_call(functools.partial(sweep_kernel, sectors, groups), out_shap...]
where the time goes in v5:
time: 166 us
  Pallas kernels  163 us (98%)
  local copies, waits for them, and re-layouts  2.71 us (2%)
    pallas_call x1, Pallas kernels, per_device_swept(): pl.pallas_call(functools.partial(sweep_kernel, sectors, groups), out_shap...  163 us

profile of v5, /device:TPU:7, one launch (start us, length us, event | category | flops | bytes accessed | tf_op | source)
XLA Modules:
  0.0 165.9 jit_solution(14391572225717549424)
XLA Ops:
  0.0 163.1 %shard_map.46 = bf16[6,256,2048]{2,1,0:T(8,128)(2,1)S(1)} custom-call(bf16[6,256,2048]{2,1,0:T(8,128)(2,1)} %start.1, f32[6]{0:T(128)} %energies.1, bf16[1,256]{1,0:T(2,128)(2,1)} %limits.1, bf16[256,1024]{1,0:T(8,128)(2,1)} %bitcast.3), custom_call_target="tpu_custom_call" | custom-call | tf_op jit(solution)/shard_map/pallas_call | solution.py:659
  163.1 2.7 %copy.6 = bf16[1,6,256,2048]{3,2,1,0:T(8,128)(2,1)} copy(bf16[1,6,256,2048]{3,2,1,0:T(8,128)(2,1)S(1)} %bitcast.2) | data formatting | bytes 12582912

commit v6 on v5

--- a/solution.py
+++ b/solution.py
@@ -75,19 +75,19 @@
 PAIRED = 2
 EXTRA = 2
 QUARTERED = (0, 1)
-HOME, LIFT, HOP, SIDE, TWIN, FEED, FEED_HOP, STEP, FAR, ANGLES, END = range(11)
+HOME, LIFT, HOP, SIDE, TWIN, FEED, FEED_HOP, STEP, FAR, ANGLES, MEET, BOUND, SPREAD, END = range(14)
 TUNED = (
-    (5, 0, 0), (5, 1, 0), (6, 1, 1), (6, 0, 1), (6, 1, 2), (5, 2, 0), (0, 2, 0), (1, 2, 0), (0, 1, 0), (1, 1, 0),
-    (0, 0, 0), (0, 3, 0), (2, 1, 1), (2, 1, 2), (1, 0, 0), (2, 1, 3), (3, 1, 1), (2, 0, 1), (2, 0, 2), (8, 1, 1),
-    (3, 1, 3), (2, 0, 3), (3, 1, 2), (1, 3, 0), (2, 2, 1), (3, 0, 3), (2, 3, 1), (2, 3, 2), (3, 0, 2), (3, 2, 1),
-    (3, 0, 1), (8, 0, 3), (8, 1, 2), (6, 0, 2), (6, 0, 3), (8, 1, 3), (2, 3, 3), (6, 1, 3), (2, 2, 2), (3, 3, 2),
-    (8, 0, 2), (8, 0, 1), (5, 7, 0), (2, 2, 3), (6, 2, 1), (5, 4, 0), (3, 3, 1), (4, 1, 0), (4, 0, 0), (7, 0, 0),
-    (3, 2, 2), (5, 3, 0), (3, 2, 3), (7, 1, 0), (7, 2, 0), (3, 3, 3), (7, 3, 0), (6, 2, 2), (4, 3, 0), (4, 2, 0),
-    (7, 4, 0), (6, 4, 1), (7, 5, 0), (7, 6, 0), (6, 3, 1), (7, 7, 0), (6, 2, 3), (6, 3, 2), (5, 5, 0), (6, 3, 3),
-    (7, 0, 1), (7, 1, 1), (7, 2, 1), (7, 3, 1), (6, 4, 2), (6, 5, 1), (7, 4, 1), (5, 6, 0), (7, 5, 1), (6, 5, 2),
-    (7, 6, 1), (6, 7, 1), (6, 5, 3), (7, 7, 1), (6, 4, 3), (6, 6, 1), (6, 7, 2), (7, 0, 2), (7, 1, 2), (6, 6, 2),
-    (7, 2, 2), (7, 3, 2), (7, 4, 2), (6, 7, 3), (6, 6, 3), (7, 5, 2), (7, 0, 3), (7, 6, 2), (7, 1, 3), (7, 2, 3),
-    (7, 7, 2), (7, 3, 3), (7, 4, 3), (7, 5, 3), (7, 6, 3), (7, 7, 3),
+    (5, 1, 0), (5, 0, 0), (6, 1, 1), (6, 0, 1), (5, 2, 0), (6, 1, 2), (0, 1, 0), (1, 1, 0), (0, 2, 0), (1, 2, 0),
+    (0, 0, 0), (0, 3, 0), (2, 1, 1), (1, 0, 0), (2, 1, 2), (2, 0, 1), (2, 1, 3), (2, 0, 2), (3, 1, 2), (6, 1, 3),
+    (6, 0, 2), (2, 0, 3), (1, 3, 0), (3, 0, 2), (3, 1, 3), (3, 0, 1), (3, 1, 1), (3, 0, 3), (2, 3, 1), (2, 2, 1),
+    (8, 1, 3), (8, 0, 2), (2, 2, 2), (8, 0, 1), (6, 0, 3), (8, 0, 3), (8, 1, 1), (8, 1, 2), (2, 3, 2), (2, 2, 3),
+    (4, 0, 0), (5, 3, 0), (3, 3, 1), (7, 0, 0), (2, 3, 3), (7, 1, 0), (3, 2, 1), (5, 4, 0), (6, 2, 1), (4, 1, 0),
+    (3, 3, 2), (6, 3, 1), (5, 5, 0), (3, 2, 2), (3, 2, 3), (3, 3, 3), (7, 2, 0), (7, 3, 0), (4, 2, 0), (7, 4, 0),
+    (7, 5, 0), (4, 3, 0), (7, 6, 0), (6, 2, 2), (7, 7, 0), (6, 3, 2), (6, 2, 3), (6, 3, 3), (7, 0, 1), (7, 1, 1),
+    (6, 5, 1), (6, 5, 2), (7, 2, 1), (7, 3, 1), (5, 6, 0), (7, 4, 1), (6, 4, 1), (7, 5, 1), (6, 6, 1), (7, 6, 1),
+    (7, 7, 1), (6, 4, 2), (6, 5, 3), (6, 4, 3), (5, 7, 0), (7, 0, 2), (7, 1, 2), (7, 2, 2), (6, 6, 2), (7, 3, 2),
+    (7, 4, 2), (6, 7, 1), (6, 7, 2), (7, 5, 2), (6, 7, 3), (6, 6, 3), (7, 0, 3), (7, 6, 2), (7, 1, 3), (7, 2, 3),
+    (7, 3, 3), (7, 4, 3), (7, 5, 3), (7, 6, 3), (7, 7, 3), (7, 7, 2),
 )
 
 
@@ -113,13 +113,15 @@
 def order_of(pairs, sectors, energy_count, groups):
     plain = plain_order(pairs, sectors, energy_count, groups)
     chosen = TUNED if sorted(TUNED) == sorted(plain) else plain
-    order, left = [], list(range(sectors))
+    order, left = [], [(MEET, 0, 0), (BOUND, 1, 0), (MEET, 1, 0)]
+    left += [(BOUND, d, 0) for d in range(2, groups)] + [(SPREAD, 0, 0)]
+    left += [(ANGLES, s, 0) for s in range(sectors)]
     for entry in chosen:
         while left and entry[0] == STEP:
-            order.append((ANGLES, left.pop(0), 0))
+            order.append(left.pop(0))
         order.append(entry)
         if left:
-            order.append((ANGLES, left.pop(0), 0))
+            order.append(left.pop(0))
     return order
 
 
@@ -137,7 +139,7 @@
     sectors, groups, start, energies, limits, own_block, out,
     basis, amps, rotated, kept, doubled, turn, bounds,
     local_sem, block_recv, column_send, row_send, up_send, down_send, core_send,
-    start_recv, start_up, start_down, bound_send, bound_recv, out_send, out_recv, out_local, doubled_sem,
+    start_recv, start_up, start_down, bound_send, bound_recv, out_send, out_recv, out_local, doubled_sem, met, spread_send, spread_recv,
 ):
     k = lax.axis_index("sec")
     z = lax.axis_index("ch")
@@ -154,7 +156,6 @@
     width = half_cols // sectors
     channel_count = row_count * groups
     chunks = channel_count // LANES
-    devices = sectors * groups
     across = column_peer + row_peer - k
     across_chip = across // 2
     shared = energy_count - EXTRA
@@ -171,10 +172,6 @@
 
     def rows_of(c):
         return pl.ds(pl.multiple_of(c * row_count, row_count), row_count)
-
-    def other(step):
-        place = (k * groups + z + step) % devices
-        return {"sec": place // groups, "ch": place % groups}
 
     def part_of(s, b, r, count=1):
         return basis.at[s, pl.ds(pl.multiple_of(b * row_count + r * piece, piece), count * piece), :]
@@ -369,32 +366,64 @@
 
     barrier = pltpu.get_barrier_semaphore()
 
-    @pl.loop(1, devices)
-    def _(step):
-        pl.semaphore_signal(barrier, inc=1, device_id=other(step), device_id_type=pl.DeviceIdType.MESH)
-
-    pl.semaphore_wait(barrier, devices - 1)
+    for near_by in (partner, column_peer, row_peer):
+        pl.semaphore_signal(barrier, inc=1, device_id={"sec": near_by}, device_id_type=pl.DeviceIdType.MESH)
+
+    @pl.when(has_up)
+    def _():
+        pl.semaphore_signal(barrier, inc=1, device_id={"ch": z + 1}, device_id_type=pl.DeviceIdType.MESH)
+
+    @pl.when(has_down)
+    def _():
+        pl.semaphore_signal(barrier, inc=1, device_id={"ch": z - 1}, device_id_type=pl.DeviceIdType.MESH)
+
+    line_peers = jnp.minimum(z, 1) + jnp.minimum(groups - 1 - z, 1)
+    pl.semaphore_wait(barrier, 3 + line_peers)
     loads[0].wait()
 
     give_own()
     for load in loads[1:]:
         load.wait()
 
-    def bound_move(step):
-        return pltpu.make_async_remote_copy(
-            src_ref=bounds.at[k, z], dst_ref=bounds.at[k, z], send_sem=bound_send.at[step], recv_sem=bound_recv.at[k, z],
-            device_id=other(step), device_id_type=pl.DeviceIdType.MESH,
-        )
-
-    @pl.loop(1, devices)
-    def _(step):
-        bound_move(step).start()
+    def bound_move(b, turned):
+        send, target = (bound_send.at[1, b], z - 1) if turned else (bound_send.at[0, b], z + 1)
+        return remote(bounds.at[k, b], bounds.at[k, b], send, bound_recv.at[b], ch=target)
+
+    def each_bound(b, action):
+        @pl.when(has_up & (b <= z))
+        def _():
+            action(bound_move(b, 0))
+
+        @pl.when(has_down & (b >= z))
+        def _():
+            action(bound_move(b, 1))
+
+    each_bound(z, lambda move: move.start())
+
+    def bound_from(d):
+        for b in (z - d, z + d):
+            @pl.when((b >= 0) & (b < groups))
+            def _():
+                bound_move(b, 0).wait_recv()
+                each_bound(b, lambda move: move.start())
+
+    def spread_move(step):
+        return remote(bounds.at[k], bounds.at[k], spread_send.at[step], spread_recv.at[k], sec=(k + step) % sectors)
+
+    def spread():
+        @pl.loop(1, sectors)
+        def _(step):
+            spread_move(step).start()
+
+    def meet(turn_of):
+        target = jnp.where(turn_of == 0, partner, column_peer)
+        pl.semaphore_signal(met.at[turn_of], inc=1, device_id={"sec": target}, device_id_type=pl.DeviceIdType.MESH)
+        pl.semaphore_wait(met.at[turn_of], 1)
 
     def angles(s):
-        for c in range(groups):
-            @pl.when((s != k) | (c != z))
-            def _():
-                remote(bounds.at[s, c], bounds.at[s, c], bound_send.at[0], bound_recv.at[s, c], sec=partner).wait_recv()
+        @pl.when(s != k)
+        def _():
+            remote(bounds.at[s], bounds.at[s], spread_send.at[0], spread_recv.at[s], sec=partner).wait_recv()
 
         floor = jnp.concatenate([bounds[s, c] for c in range(groups)], axis=0)
         wavenumber = jnp.concatenate([jnp.sqrt(energies[e] - floor) for e in range(energy_count)], axis=0)
@@ -541,6 +570,18 @@
         def _():
             side_from(first, second)
 
+        @pl.when(kind == MEET)
+        def _():
+            meet(first)
+
+        @pl.when(kind == BOUND)
+        def _():
+            bound_from(first)
+
+        @pl.when(kind == SPREAD)
+        def _():
+            spread()
+
         @pl.when(kind == FAR)
         def _():
             far_from(first, second)
@@ -574,9 +615,12 @@
 
     lax.fori_loop(0, len(codes), act, (jnp.int32(END),) + (jnp.int32(0),) * 4)
 
-    @pl.loop(1, devices)
+    for b in range(groups):
+        each_bound(b, lambda move: move.wait_send())
+
+    @pl.loop(1, sectors)
     def _(step):
-        bound_move(step).wait_send()
+        spread_move(step).wait_send()
 
     def drain(send, s, b, count, **where):
         part = part_of(s, 0, 0, count)
@@ -684,12 +728,15 @@
             dma((energy_count + EXTRA, groups)),
             dma((groups,)),
             dma((groups,)),
-            dma((sectors * groups,)),
-            dma((sectors, groups)),
+            dma((2, groups)),
+            dma((groups,)),
             dma((sectors,)),
             dma((sectors,)),
             dma((1,)),
             dma((3,)),
+            pltpu.SemaphoreType.REGULAR((2,)),
+            dma((sectors,)),
+            dma((sectors,)),
         ],
         compiler_params=pltpu.CompilerParams(
             collective_id=0, has_side_effects=True, vmem_limit_bytes=56 * 2**20

time: 166 us -> 157 us (0.946)
  Pallas kernels: 163 us -> 154 us
    pallas_call x1, Pallas kernels: 163 us -> 154 us  [per_device_swept(): pl.pallas_call(functools.partial(sweep_kernel, sectors, groups), out_shap...]
where the time goes in v6:
time: 157 us; the launch traced here: 156 us
  Pallas kernels  154 us (98%)
  local copies, waits for them, and re-layouts  2.71 us (2%)
    pallas_call x1, Pallas kernels, per_device_swept(): pl.pallas_call(functools.partial(sweep_kernel, sectors, groups), out_shap...  154 us

profile of v6, /device:TPU:7, one launch (start us, length us, event | category | flops | bytes accessed | tf_op | source)
XLA Modules:
  0.0 156.4 jit_solution(15546145701568237093)
XLA Ops:
  0.0 153.7 %shard_map.46 = bf16[6,256,2048]{2,1,0:T(8,128)(2,1)S(1)} custom-call(bf16[6,256,2048]{2,1,0:T(8,128)(2,1)} %start.1, f32[6]{0:T(128)} %energies.1, bf16[1,256]{1,0:T(2,128)(2,1)} %limits.1, bf16[256,1024]{1,0:T(8,128)(2,1)} %bitcast.3), custom_call_target="tpu_custom_call" | custom-call | tf_op jit(solution)/shard_map/pallas_call | solution.py:703
  153.7 2.7 %copy.6 = bf16[1,6,256,2048]{3,2,1,0:T(8,128)(2,1)} copy(bf16[1,6,256,2048]{3,2,1,0:T(8,128)(2,1)S(1)} %bitcast.2) | data formatting | bytes 12582912

commit v7 on v6

--- a/solution.py
+++ b/solution.py
@@ -77,17 +77,17 @@
 QUARTERED = (0, 1)
 HOME, LIFT, HOP, SIDE, TWIN, FEED, FEED_HOP, STEP, FAR, ANGLES, MEET, BOUND, SPREAD, END = range(14)
 TUNED = (
-    (5, 1, 0), (5, 0, 0), (6, 1, 1), (6, 0, 1), (5, 2, 0), (6, 1, 2), (0, 1, 0), (1, 1, 0), (0, 2, 0), (1, 2, 0),
-    (0, 0, 0), (0, 3, 0), (2, 1, 1), (1, 0, 0), (2, 1, 2), (2, 0, 1), (2, 1, 3), (2, 0, 2), (3, 1, 2), (6, 1, 3),
-    (6, 0, 2), (2, 0, 3), (1, 3, 0), (3, 0, 2), (3, 1, 3), (3, 0, 1), (3, 1, 1), (3, 0, 3), (2, 3, 1), (2, 2, 1),
-    (8, 1, 3), (8, 0, 2), (2, 2, 2), (8, 0, 1), (6, 0, 3), (8, 0, 3), (8, 1, 1), (8, 1, 2), (2, 3, 2), (2, 2, 3),
-    (4, 0, 0), (5, 3, 0), (3, 3, 1), (7, 0, 0), (2, 3, 3), (7, 1, 0), (3, 2, 1), (5, 4, 0), (6, 2, 1), (4, 1, 0),
-    (3, 3, 2), (6, 3, 1), (5, 5, 0), (3, 2, 2), (3, 2, 3), (3, 3, 3), (7, 2, 0), (7, 3, 0), (4, 2, 0), (7, 4, 0),
-    (7, 5, 0), (4, 3, 0), (7, 6, 0), (6, 2, 2), (7, 7, 0), (6, 3, 2), (6, 2, 3), (6, 3, 3), (7, 0, 1), (7, 1, 1),
-    (6, 5, 1), (6, 5, 2), (7, 2, 1), (7, 3, 1), (5, 6, 0), (7, 4, 1), (6, 4, 1), (7, 5, 1), (6, 6, 1), (7, 6, 1),
-    (7, 7, 1), (6, 4, 2), (6, 5, 3), (6, 4, 3), (5, 7, 0), (7, 0, 2), (7, 1, 2), (7, 2, 2), (6, 6, 2), (7, 3, 2),
-    (7, 4, 2), (6, 7, 1), (6, 7, 2), (7, 5, 2), (6, 7, 3), (6, 6, 3), (7, 0, 3), (7, 6, 2), (7, 1, 3), (7, 2, 3),
-    (7, 3, 3), (7, 4, 3), (7, 5, 3), (7, 6, 3), (7, 7, 3), (7, 7, 2),
+    (5, 1, 0), (5, 0, 0), (6, 1, 1), (6, 0, 1), (6, 1, 2), (5, 2, 0), (0, 1, 0), (1, 1, 0), (0, 2, 0), (1, 2, 0),
+    (0, 3, 0), (0, 0, 0), (2, 1, 1), (1, 0, 0), (2, 1, 2), (2, 0, 1), (2, 1, 3), (2, 0, 2), (3, 1, 2), (1, 3, 0),
+    (2, 0, 3), (3, 1, 3), (2, 3, 1), (3, 0, 3), (3, 0, 1), (6, 0, 2), (3, 0, 2), (3, 1, 1), (2, 2, 1), (8, 0, 3),
+    (6, 0, 3), (8, 1, 2), (2, 2, 2), (8, 0, 2), (8, 1, 3), (8, 0, 1), (2, 2, 3), (2, 3, 2), (3, 3, 1), (6, 1, 3),
+    (8, 1, 1), (4, 0, 0), (5, 3, 0), (7, 0, 0), (2, 3, 3), (7, 1, 0), (3, 2, 1), (6, 2, 1), (3, 2, 3), (3, 2, 2),
+    (4, 1, 0), (7, 2, 0), (6, 3, 1), (7, 3, 0), (3, 3, 3), (3, 3, 2), (5, 4, 0), (5, 5, 0), (4, 2, 0), (7, 4, 0),
+    (7, 5, 0), (4, 3, 0), (7, 6, 0), (6, 3, 2), (7, 7, 0), (6, 2, 2), (6, 2, 3), (6, 3, 3), (7, 0, 1), (7, 1, 1),
+    (5, 6, 0), (6, 4, 1), (7, 2, 1), (6, 5, 1), (7, 3, 1), (7, 4, 1), (6, 4, 2), (7, 5, 1), (6, 5, 2), (7, 6, 1),
+    (6, 4, 3), (5, 7, 0), (6, 6, 1), (6, 5, 3), (7, 0, 2), (7, 1, 2), (7, 7, 1), (6, 7, 1), (7, 2, 2), (6, 6, 2),
+    (7, 3, 2), (6, 7, 2), (7, 4, 2), (7, 5, 2), (6, 6, 3), (7, 6, 2), (6, 7, 3), (7, 0, 3), (7, 1, 3), (7, 2, 3),
+    (7, 3, 3), (7, 7, 2), (7, 4, 3), (7, 5, 3), (7, 6, 3), (7, 7, 3),
 )
 
 

time: 157 us -> 151 us (0.962)
  Pallas kernels: 154 us -> 148 us
    pallas_call x1, Pallas kernels: 154 us -> 148 us  [per_device_swept(): pl.pallas_call(functools.partial(sweep_kernel, sectors, groups), out_shap...]
where the time goes in v7:
time: 151 us; the launch traced here: 150 us
  Pallas kernels  148 us (98%)
  local copies, waits for them, and re-layouts  2.71 us (2%)
    pallas_call x1, Pallas kernels, per_device_swept(): pl.pallas_call(functools.partial(sweep_kernel, sectors, groups), out_shap...  148 us

profile of v7, /device:TPU:7, one launch (start us, length us, event | category | flops | bytes accessed | tf_op | source)
XLA Modules:
  0.0 150.4 jit_solution(13484808436140896416)
XLA Ops:
  0.0 147.7 %shard_map.46 = bf16[6,256,2048]{2,1,0:T(8,128)(2,1)S(1)} custom-call(bf16[6,256,2048]{2,1,0:T(8,128)(2,1)} %start.1, f32[6]{0:T(128)} %energies.1, bf16[1,256]{1,0:T(2,128)(2,1)} %limits.1, bf16[256,1024]{1,0:T(8,128)(2,1)} %bitcast.3), custom_call_target="tpu_custom_call" | custom-call | tf_op jit(solution)/shard_map/pallas_call | solution.py:703
  147.7 2.7 %copy.6 = bf16[1,6,256,2048]{3,2,1,0:T(8,128)(2,1)} copy(bf16[1,6,256,2048]{3,2,1,0:T(8,128)(2,1)S(1)} %bitcast.2) | data formatting | bytes 12582912

commit v8 on v7

--- a/solution.py
+++ b/solution.py
@@ -739,7 +739,7 @@
             dma((sectors,)),
         ],
         compiler_params=pltpu.CompilerParams(
-            collective_id=0, has_side_effects=True, vmem_limit_bytes=56 * 2**20
+            collective_id=0, has_side_effects=True, vmem_limit_bytes=115 * 2**19
         ),
     )(start_amps, energies, thresholds, intersection[0])
     return swept[None]

time: 151 us -> 151 us (level)
  no operation moved by 1% of the time
where the time goes in v8:
time: 151 us; the launch traced here: 150 us
  Pallas kernels  148 us (98%)
  local copies, waits for them, and re-layouts  2.71 us (2%)
    pallas_call x1, Pallas kernels, per_device_swept(): pl.pallas_call(functools.partial(sweep_kernel, sectors, groups), out_shap...  148 us

profile of v8, /device:TPU:7, one launch (start us, length us, event | category | flops | bytes accessed | tf_op | source)
XLA Modules:
  0.0 150.4 jit_solution(3324803613245050345)
XLA Ops:
  0.0 147.7 %shard_map.46 = bf16[6,256,2048]{2,1,0:T(8,128)(2,1)S(1)} custom-call(bf16[6,256,2048]{2,1,0:T(8,128)(2,1)} %start.1, f32[6]{0:T(128)} %energies.1, bf16[1,256]{1,0:T(2,128)(2,1)} %limits.1, bf16[256,1024]{1,0:T(8,128)(2,1)} %bitcast.3), custom_call_target="tpu_custom_call" | custom-call | tf_op jit(solution)/shard_map/pallas_call | solution.py:703
  147.7 2.7 %copy.6 = bf16[1,6,256,2048]{3,2,1,0:T(8,128)(2,1)} copy(bf16[1,6,256,2048]{3,2,1,0:T(8,128)(2,1)S(1)} %bitcast.2) | data formatting | bytes 12582912
